TPU v7x, 256 devices: a whole 4x4x8 slice. The times are simulated.
256 devices in a mesh: dp: 4 (over y_lo, core), tile: 64 (over y_hi, x, z).
Axes of the slice: x: 4, y: 4 (y_hi: 2, y_lo: 2; y = y_hi * 2 + y_lo), z: 8, core: 2. Of those that a mesh axis runs over, the one named last changes fastest.
Arguments:
- inputs: bfloat16 [8, 64, 1024, 256], P('dp', None, 'tile'), may hold values from -6 to 6
- cotangent: bfloat16 [8, 64, 1024, 256], P('dp', None, 'tile'), may hold values from -6 to 6
- mode_weight: bfloat16 [64, 64, 64, 128], P('tile'), may hold values from -0.5 to 0.5
- local_weight: bfloat16 [64, 64], replicated, may hold values from -0.75 to 0.75
Outputs:
- input_grad: bfloat16 [8, 64, 1024, 256], P('dp', None, 'tile')
- mode_grad: float32 [64, 64, 64, 128], P('tile')
- local_grad: float32 [64, 64], replicated
All inputs are finite; a program needn't handle non-finite values.
Results may differ from a plain program's by a relative error of at most 0.015.
Values may be sent and summed in bfloat16 or wider, within the bound.
A program may use at most 64 MiB of HBM per device.

v0:
```python
import functools
import math

import jax
import jax.numpy as jnp
from jax import lax
from jax.sharding import Mesh
from jax.sharding import PartitionSpec as P

C = 64
M1 = 64
M2 = 64
W = 256
TH = 16
TILE = ("tile_0", "tile_1", "tile_2")
DP = ("dp_0", "dp_1")
DP_TILE = ("dp_0", "dp_1", "tile_0", "tile_1", "tile_2")


def one_axis_at_a_time(value, axes):
    return functools.reduce(lax.psum, axes, value)


def row_tables(positions, length):
    modes = jnp.arange(M1, dtype=jnp.int32)
    signed = jnp.where(modes < M1 // 2, modes, modes - M1)
    phases = jnp.mod(positions[:, None] * signed[None, :], length)
    angles = phases.astype(jnp.float32) * (2.0 * math.pi / length)
    return jnp.concatenate([jnp.cos(angles), jnp.sin(angles)], axis=1).astype(jnp.bfloat16)


def column_tables():
    modes = jnp.arange(M2, dtype=jnp.int32)
    pixels = jnp.arange(W, dtype=jnp.int32)
    phases = jnp.mod(modes[:, None] * pixels[None, :], W)
    angles = phases.astype(jnp.float32) * (2.0 * math.pi / W)
    return jnp.concatenate([jnp.cos(angles), -jnp.sin(angles)], axis=0).astype(jnp.bfloat16)


def inverse_rows(tables):
    cosine = tables[:, :M1]
    sine = tables[:, M1:]
    upper = jnp.concatenate([cosine.T, sine.T], axis=1)
    lower = jnp.concatenate([-sine.T, cosine.T], axis=1)
    return jnp.concatenate([upper, lower], axis=0)


def along_rows(halves, tables):
    mixed = jnp.einsum("pqsch,hm->pqscm", halves, tables, preferred_element_type=jnp.float32)
    real_part = mixed[0]
    imag_part = mixed[1]
    return jnp.concatenate(
        [real_part[..., :M1] + imag_part[..., M1:], imag_part[..., :M1] - real_part[..., M1:]],
        axis=-1,
    )


def products(left, right, form):
    return jnp.einsum(form, left, right, preferred_element_type=jnp.float32)


def mix_forward(spectra, weights):
    real_in, imag_in = (spectra[..., :M1], spectra[..., M1:])
    real_w, imag_w = (weights[..., :M1], weights[..., M1:])
    form = "qsck,qcok->qsok"
    real_out = products(real_in, real_w, form) - products(imag_in, imag_w, form)
    imag_out = products(real_in, imag_w, form) + products(imag_in, real_w, form)
    return jnp.concatenate([real_out, imag_out], axis=-1)


def mix_backward(grads, weights):
    real_g, imag_g = (grads[..., :M1], grads[..., M1:])
    real_w, imag_w = (weights[..., :M1], weights[..., M1:])
    form = "qsok,qcok->qsck"
    real_out = products(real_g, real_w, form) + products(imag_g, imag_w, form)
    imag_out = products(imag_g, real_w, form) - products(real_g, imag_w, form)
    return jnp.concatenate([real_out, imag_out], axis=-1)


def weight_term(spectra, grads):
    real_in, imag_in = (spectra[..., :M1], spectra[..., M1:])
    real_g, imag_g = (grads[..., :M1], grads[..., M1:])
    form = "qsck,qsok->qcok"
    real_out = products(real_in, real_g, form) + products(imag_in, imag_g, form)
    imag_out = products(real_in, imag_g, form) - products(imag_in, real_g, form)
    return jnp.concatenate([real_out, imag_out], axis=-1)


def gelu_slope(values):
    cumulative = 0.5 * (1.0 + jax.scipy.special.erf(values / math.sqrt(2.0)))
    density = jnp.exp(-0.5 * values * values) / math.sqrt(2.0 * math.pi)
    return cumulative + values * density


def local(inputs, cotangent, mode_weight, local_weight):
    parts = lax.axis_size(TILE)
    height = TH * parts
    owned = mode_weight.shape[0]
    spec_scale = 1.0 / math.sqrt(height * W)
    mode_scale = 1.0 / math.sqrt(M1 * M2)
    col_table = column_tables()
    col_three = col_table.reshape(2, M2, W)
    full_rows = row_tables(jnp.arange(height, dtype=jnp.int32), height)
    full_back = inverse_rows(full_rows)

    def to_owners(fields, scale):
        samples = fields.shape[0]
        halves = products(col_table, fields, "qw,schw->qsch").astype(jnp.bfloat16)
        halves = halves.reshape(2, M2, samples, C, TH)
        whole = lax.all_to_all(halves, TILE, split_axis=1, concat_axis=4, tiled=True)
        return (scale * along_rows(whole, full_rows)).astype(jnp.bfloat16)

    def to_pixels(spectra, scale):
        samples = spectra.shape[1]
        inner = products(spectra, full_back, "qsom,mj->qsoj").astype(jnp.bfloat16)
        inner = inner.reshape(owned, samples, C, 2, height)
        gathered = lax.all_to_all(inner, TILE, split_axis=4, concat_axis=0, tiled=True)
        return scale * products(gathered, col_three, "qsoph,pqw->sohw")

    spectra = to_owners(inputs, spec_scale)
    outputs = mix_forward(spectra, mode_weight).astype(jnp.bfloat16)
    pre = to_pixels(outputs, mode_scale) + products(local_weight, inputs, "co,schw->sohw")
    gate_grad = (cotangent.astype(jnp.float32) * gelu_slope(pre)).astype(jnp.bfloat16)
    local_term = products(inputs, gate_grad, "schw,sohw->co")
    back_local = products(local_weight, gate_grad, "co,sohw->schw")
    out_grad = to_owners(gate_grad, mode_scale)
    in_grad = mix_backward(out_grad, mode_weight).astype(jnp.bfloat16)
    mode_term = weight_term(spectra, out_grad)
    result = (to_pixels(in_grad, spec_scale) + back_local).astype(jnp.bfloat16)
    groups = [(result, mode_term, local_term)]
    input_grad = jnp.concatenate([group[0] for group in groups], axis=0)
    mode_sum = groups[0][1]
    local_sum = groups[0][2]
    mode_grad = lax.psum(mode_sum.astype(jnp.bfloat16), DP).astype(jnp.float32)
    local_grad = one_axis_at_a_time(local_sum, DP_TILE)
    return (input_grad, mode_grad, local_grad)


def solution(mesh):
    finer = Mesh(
        mesh.devices.reshape(2, 2, 2, 4, 8), ("dp_0", "dp_1", "tile_0", "tile_1", "tile_2")
    )
    in_specs = (P(DP, None, TILE, None), P(DP, None, TILE, None), P(TILE, None, None, None), P())
    out_specs = (P(DP, None, TILE, None), P(TILE, None, None, None), P())
    return jax.shard_map(local, mesh=finer, in_specs=in_specs, out_specs=out_specs, check_vma=False)
```

profile of v0, /device:TPU:8, one launch (start us, length us, event | category | flops | bytes accessed | tf_op | source)
XLA Modules:
  0.0 237.5 jit_solution(12630425433033588046)
XLA Ops:
  7.5 1.7 convolution_convert_fusion.3
  11.0 1.5 reshape.255
  12.5 14.1 %all-to-all-start = ((bf16[64,2,2048]{2,1,0:T(2,128)(2,1)}), bf16[64,2,2048]{2,1,0:T(2,128)(2,1)}, u32[]{:S(2)}, u32[]{:S(2)}) async-start(bf16[64,2,2048]{2,1,0:T(2,128)(2,1)} %reshape.255), calls=%async_computation | async-start | bytes 1048576 | tf_op jit(solution)/shard_map/all_to_all | solution.py:110
  27.1 1.6 copy.147
  28.8 1.6 copy.148
  30.5 2.7 %fusion.47 = bf16[64,1024]{0,1:T(8,128)(2,1)} fusion(s32[64]{0:T(128)S(1)} %compare_select_fusion), kind=kLoop, calls=%fused_computation.75 | loop fusion | flops 1179648 | bytes 131328 | tf_op jit(solution)/shard_map/neg | solution.py:44
  33.1 3.0 %cosine_convert_fusion = (bf16[1024,64]{1,0:T(8,128)(2,1)S(1)}, bf16[64,1024]{0,1:T(8,128)(2,1)}, bf16[64,1024]{0,1:T(8,128)(2,1)}, bf16[1024,64]{1,0:T(8,128)(2,1)}) fusion(s32[64]{0:T(128)S(1)} %compare_select_fusion), kind=kLoop, calls=%fused_computation.64 | loop fusion | flops 1048576 | bytes 524544 | tf_op jit(solution)/shard_map/slice | solution.py:41
  36.1 10.3 %all-to-all-done = bf16[64,2,2048]{2,1,0:T(2,128)(2,1)} async-done(((bf16[64,2,2048]{2,1,0:T(2,128)(2,1)}), bf16[64,2,2048]{2,1,0:T(2,128)(2,1)}, u32[]{:S(2)}, u32[]{:S(2)}) %all-to-all-start) | async-done | bytes 524320 | tf_op jit(solution)/shard_map/all_to_all | solution.py:110
  46.4 2.3 reshape.256
  54.0 2.7 %copy.95 = bf16[1,2,64,2,1024]{2,3,1,0,4:T(2,128)(2,1)S(1)} copy(bf16[1,2,64,2,1024]{4,3,2,1,0:T(2,128)(2,1)} %reshape.239) | data formatting | bytes 1048576 | tf_op jit(solution)/shard_map/reshape | solution.py:116
  56.7 1.5 reshape.257
  58.2 5.4 %all-to-all-start.1 = ((bf16[64,2,2048]{2,1,0:T(2,128)(2,1)}), bf16[64,2,2048]{2,1,0:T(2,128)(2,1)S(1)}, u32[]{:S(2)}, u32[]{:S(2)}) async-start(bf16[64,2,2048]{2,1,0:T(2,128)(2,1)} %reshape.257), calls=%async_computation.1 | async-start | bytes 1048576 | tf_op jit(solution)/shard_map/all_to_all | solution.py:117
  64.3 1.8 fusion.36
  66.1 16.6 %all-to-all-done.1 = bf16[64,2,2048]{2,1,0:T(2,128)(2,1)S(1)} async-done(((bf16[64,2,2048]{2,1,0:T(2,128)(2,1)}), bf16[64,2,2048]{2,1,0:T(2,128)(2,1)S(1)}, u32[]{:S(2)}, u32[]{:S(2)}) %all-to-all-start.1) | async-done | bytes 524320 | tf_op jit(solution)/shard_map/all_to_all | solution.py:117
  83.4 2.4 %copy.97 = bf16[1,2,64,2,64,16]{4,5,3,2,1,0:T(8,128)(2,1)S(1)} copy(bf16[1,2,64,2,64,16]{2,3,1,5,4,0:T(2,128)(2,1)S(1)} %bitcast.192) | data formatting | bytes 1048576 | tf_op jit(solution)/shard_map/all_to_all | solution.py:117
  85.8 3.7 %fusion.5 = bf16[2,64,16,256]{3,2,1,0:T(8,128)(2,1)S(1)} fusion(f32[2,16,256,64]{2,3,1,0:T(8,128)} %fusion.36, bf16[2,64,16,256]{3,2,1,0:T(8,128)(2,1)} %param.5, bf16[2,64,256,1,1]{2,1,0,4,3:T(8,128)(2,1)} %bitcast.197, bf16[1,2,64,2,64,16]{4,5,3,2,1,0:T(8,128)(2,1)S(1)} %copy.97), kind=kOutput, calls=%fused_computation.8 | convolution fusion | flops 141033472 | bytes 4784128 | tf_op jit(solution)/shard_map/qsoph,pqw->sohw/dot_general | solution.py:59
  93.5 24.1 %all_to_all.66 = bf16[64,2,2048]{2,1,0:T(2,128)(2,1)S(1)} all-to-all(bf16[64,2,2048]{2,1,0:T(2,128)(2,1)S(1)} %reshape.259), channel_id=1, replica_groups=mesh['dp_0'=2,'dp_1'=2,'tile_0'=2,'tile_1'=4,'tile_2'=8] {'tile_0','tile..., dimensions={0} | all-to-all | bytes 1048576 | tf_op jit(solution)/shard_map/all_to_all | solution.py:110
  122.0 1.8 fusion.70
  126.9 2.6 %copy.111 = bf16[1,2,64,2,1024]{2,3,1,0,4:T(2,128)(2,1)S(1)} copy(bf16[1,2,64,2,1024]{4,3,2,1,0:T(2,128)(2,1)} %reshape.244) | data formatting | bytes 1048576 | tf_op jit(solution)/shard_map/reshape | solution.py:116
  129.5 1.6 reshape.261
  131.1 5.6 %all-to-all-start.3 = ((bf16[64,2,2048]{2,1,0:T(2,128)(2,1)}), bf16[64,2,2048]{2,1,0:T(2,128)(2,1)}, u32[]{:S(2)}, u32[]{:S(2)}) async-start(bf16[64,2,2048]{2,1,0:T(2,128)(2,1)} %reshape.261), calls=%async_computation.3 | async-start | bytes 1048576 | tf_op jit(solution)/shard_map/all_to_all | solution.py:117
  139.0 1.7 pad_maximum_fusion
  143.5 8.3 %psum.43 = f32[64,64]{0,1:T(8,128)S(1)} all-reduce(f32[64,64]{0,1:T(8,128)S(1)} %convolution_bitcast_fusion), channel_id=1, replica_groups=mesh['dp_0'=2,'dp_1'=2,'tile_0'=2,'tile_1'=4,'tile_2'=8] {'dp_0'}, use_global_device_ids=true, to_apply=%region_1.2 | all-reduce | flops 4096 | bytes 32768 | tf_op jit(solution)/shard_map/psum | solution.py:21
  151.8 3.4 %psum.44 = f32[64,64]{0,1:T(8,128)S(1)} all-reduce(f32[64,64]{0,1:T(8,128)S(1)} %psum.43), channel_id=1, replica_groups=mesh['dp_0'=2,'dp_1'=2,'tile_0'=2,'tile_1'=4,'tile_2'=8] {'dp_1'}, use_global_device_ids=true, to_apply=%region_2.3 | all-reduce | flops 4096 | bytes 32768 | tf_op jit(solution)/shard_map/psum | solution.py:21
  155.2 11.9 %psum.45 = f32[64,64]{0,1:T(8,128)S(1)} all-reduce(f32[64,64]{0,1:T(8,128)S(1)} %psum.44), channel_id=1, replica_groups=mesh['dp_0'=2,'dp_1'=2,'tile_0'=2,'tile_1'=4,'tile_2'=8] {'tile_0'}, use_global_device_ids=true, to_apply=%region_3.4 | all-reduce | flops 4096 | bytes 32768 | tf_op jit(solution)/shard_map/psum | solution.py:21
  167.1 16.8 %psum.46 = f32[64,64]{0,1:T(8,128)S(1)} all-reduce(f32[64,64]{0,1:T(8,128)S(1)} %psum.45), channel_id=1, replica_groups=mesh['dp_0'=2,'dp_1'=2,'tile_0'=2,'tile_1'=4,'tile_2'=8] {'tile_1'}, use_global_device_ids=true, to_apply=%region_4.5 | all-reduce | flops 4096 | bytes 32768 | tf_op jit(solution)/shard_map/psum | solution.py:21
  183.9 29.7 %psum.47 = f32[64,64]{0,1:T(8,128)S(1)} all-reduce(f32[64,64]{0,1:T(8,128)S(1)} %psum.46), channel_id=1, replica_groups=mesh['dp_0'=2,'dp_1'=2,'tile_0'=2,'tile_1'=4,'tile_2'=8] {'tile_2'}, use_global_device_ids=true, to_apply=%region_5.6 | all-reduce | flops 4096 | bytes 32768 | tf_op jit(solution)/shard_map/psum | solution.py:21
  214.3 1.7 fusion.33
  216.1 3.7 %reshape.262 = bf16[1024,1,2,2,64]{4,3,2,1,0:T(2,128)(2,1)} reshape(bf16[64,2,2048]{2,1,0:T(2,128)(2,1)} %all-to-all-done.3) | data formatting | bytes 1048576
  219.8 3.2 %copy.113 = bf16[1,2,64,2,64,16]{4,5,3,2,1,0:T(8,128)(2,1)S(1)} copy(bf16[1,2,64,2,64,16]{2,3,1,5,4,0:T(2,128)(2,1)} %bitcast.194) | data formatting | bytes 1048576 | tf_op jit(solution)/shard_map/all_to_all | solution.py:117
  223.0 2.4 %fusion.6 = bf16[2,64,16,256]{3,2,1,0:T(8,128)(2,1)} fusion(f32[2,16,256,64]{2,3,1,0:T(8,128)S(1)} %fusion.33, bf16[2,64,256,1,1]{2,1,0,4,3:T(8,128)(2,1)S(1)} %bitcast.198, bf16[1,2,64,2,64,16]{4,5,3,2,1,0:T(8,128)(2,1)S(1)} %copy.113), kind=kOutput, calls=%fused_computation.11 | convolution fusion | flops 135790592 | bytes 3735552 | tf_op jit(solution)/shard_map/qsoph,pqw->sohw/dot_general | solution.py:59
  225.4 5.3 %copy.126 = f32[1,64,64,128]{3,2,1,0:T(8,128)} copy(bf16[1,64,64,128]{1,2,3,0:T(8,128)(2,1)} %all-reduce.2.cloned.1.call-done) | data formatting | bytes 3145728
  (87 shorter events, 26.3 us)
Async XLA Ops:
  7.2 57.1 %copy-start = (bf16[64,64]{1,0:T(8,128)(2,1)S(1)}, bf16[64,64]{1,0:T(8,128)(2,1)}, u32[]{:S(2)}) copy-start(bf16[64,64]{1,0:T(8,128)(2,1)} %param.7) | copy-start | bytes 24580
  9.6 17.0 %copy-start.6 = (bf16[1,64,64,128]{3,2,1,0:T(8,128)(2,1)S(1)}, bf16[1,64,64,128]{3,2,1,0:T(8,128)(2,1)}, u32[]{:S(2)}) copy-start(bf16[1,64,64,128]{3,2,1,0:T(8,128)(2,1)} %param.6) | copy-start | bytes 3145732
  12.5 33.9 %all-to-all-start = ((bf16[64,2,2048]{2,1,0:T(2,128)(2,1)}), bf16[64,2,2048]{2,1,0:T(2,128)(2,1)}, u32[]{:S(2)}, u32[]{:S(2)}) async-start(bf16[64,2,2048]{2,1,0:T(2,128)(2,1)} %reshape.255), calls=%async_computation | async-start | bytes 1048576 | tf_op jit(solution)/shard_map/all_to_all | solution.py:110
  30.4 21.0 %copy-start.7 = (bf16[1,64,64,64]{2,1,3,0:T(8,128)(2,1)}, bf16[1,64,64,64]{2,1,3,0:T(8,128)(2,1)S(1)}, u32[]{:S(2)}) copy-start(bf16[1,64,64,64]{2,1,3,0:T(8,128)(2,1)S(1)} %copy.148) | copy-start | bytes 1572868
  48.7 1.0 copy-start.9
  51.1 1.3 copy-start.11
  51.1 1.3 copy-start.13
  51.1 1.3 copy-start.15
  54.0 10.2 %copy-start.2 = (bf16[2,64,16,256]{3,2,1,0:T(8,128)(2,1)S(1)}, bf16[2,64,16,256]{3,2,1,0:T(8,128)(2,1)}, u32[]{:S(2)}) copy-start(bf16[2,64,16,256]{3,2,1,0:T(8,128)(2,1)} %param.4) | copy-start | bytes 3145732
  58.2 24.4 %all-to-all-start.1 = ((bf16[64,2,2048]{2,1,0:T(2,128)(2,1)}), bf16[64,2,2048]{2,1,0:T(2,128)(2,1)S(1)}, u32[]{:S(2)}, u32[]{:S(2)}) async-start(bf16[64,2,2048]{2,1,0:T(2,128)(2,1)} %reshape.257), calls=%async_computation.1 | async-start | bytes 1048576 | tf_op jit(solution)/shard_map/all_to_all | solution.py:117
  89.5 1.0 copy-start.4
  118.2 1.0 copy-start.10
  121.3 2.5 %copy-start.8 = (bf16[1,64,64,64]{2,1,3,0:T(8,128)(2,1)S(1)}, bf16[1,64,64,64]{2,1,3,0:T(8,128)(2,1)}, u32[]{:S(2)}) copy-start(bf16[1,64,64,64]{2,1,3,0:T(8,128)(2,1)} %copy-done.7) | copy-start | bytes 1572868
  122.0 3.3 %copy-start.12 = (bf16[64,1024]{0,1:T(8,128)(2,1)S(1)}, bf16[64,1024]{0,1:T(8,128)(2,1)}, u32[]{:S(2)}) copy-start(bf16[64,1024]{0,1:T(8,128)(2,1)} %fusion.47) | copy-start | bytes 393220
  122.0 3.3 %copy-start.14 = (bf16[64,1024]{0,1:T(8,128)(2,1)S(1)}, bf16[64,1024]{0,1:T(8,128)(2,1)}, u32[]{:S(2)}) copy-start(bf16[64,1024]{0,1:T(8,128)(2,1)} %get-tuple-element.23) | copy-start | bytes 393220
  122.0 3.3 %copy-start.16 = (bf16[64,1024]{0,1:T(8,128)(2,1)S(1)}, bf16[64,1024]{0,1:T(8,128)(2,1)}, u32[]{:S(2)}) copy-start(bf16[64,1024]{0,1:T(8,128)(2,1)} %get-tuple-element.24) | copy-start | bytes 393220
  131.1 85.0 %all-to-all-start.3 = ((bf16[64,2,2048]{2,1,0:T(2,128)(2,1)}), bf16[64,2,2048]{2,1,0:T(2,128)(2,1)}, u32[]{:S(2)}, u32[]{:S(2)}) async-start(bf16[64,2,2048]{2,1,0:T(2,128)(2,1)} %reshape.261), calls=%async_computation.3 | async-start | bytes 1048576 | tf_op jit(solution)/shard_map/all_to_all | solution.py:117
  136.6 88.8 %all-reduce.2.cloned.1.call-start = ((), (), s32[]{:S(2)}) async-start(), calls=%async_computation.4 | async-start | bytes 4194304 | tf_op jit(solution)/shard_map/psum | solution.py:134
  137.0 1.6 copy-start.1
  140.8 1.2 copy-start.3
  140.8 1.5 copy-start.5
  216.1 7.0 %copy-start.17 = (bf16[128,256]{1,0:T(8,128)(2,1)S(1)}, bf16[128,256]{1,0:T(8,128)(2,1)}, u32[]{:S(2)}) copy-start(bf16[128,256]{1,0:T(8,128)(2,1)} %maximum_convert_fusion) | copy-start | bytes 196612
Sparse Core Ops, SparseCore 0:
  140.9 63.4 all-reduce.1
where the time goes:
time: 238 us
  blocking collectives  94.1 us (40%)
  local copies, waits for them, and re-layouts  45.2 us (19%)
  waiting for transfers between devices  26.9 us (11%)
  starting transfers between devices  25.4 us (11%)
  matrix products  22.5 us (9%)
  between operations  14.6 us (6%)
  other arithmetic  8.89 us (4%)
    psum x5, blocking collectives, one_axis_at_a_time(): return functools.reduce(lax.psum, axes, value)  70.1 us
    unnamed x48, local copies, waits for them, and re-layouts  26.9 us
    all_to_all x1, blocking collectives, to_owners(): lax.all_to_all(halves, TILE, split_axis=1, concat_axis=4, tiled=True)  24.1 us
    dot_general x21, matrix products, products(): return jnp.einsum(form, left, right, preferred_element_type=jnp.float32)  21.4 us
    all_to_all x2, waiting for transfers between devices, to_pixels(): lax.all_to_all(inner, TILE, split_axis=4, concat_axis=0, tiled=True)  16.6 us
    all_to_all x1, starting transfers between devices, to_owners(): lax.all_to_all(halves, TILE, split_axis=1, concat_axis=4, tiled=True)  14.1 us
    all_to_all x2, starting transfers between devices, to_pixels(): lax.all_to_all(inner, TILE, split_axis=4, concat_axis=0, tiled=True)  10.9 us
    all_to_all x1, waiting for transfers between devices, to_owners(): lax.all_to_all(halves, TILE, split_axis=1, concat_axis=4, tiled=True)  10.3 us
  transfers between devices with their start and end apart: 4, of which 2 were waited for; matrix products, arithmetic and copies ran while one was open for 12% of the time, Pallas kernels for 0%

commit v1 on v0

--- a/solution.py
+++ b/solution.py
@@ -1,4 +1,3 @@
-import functools
 import math
 
 import jax
@@ -15,10 +14,6 @@
 TILE = ("tile_0", "tile_1", "tile_2")
 DP = ("dp_0", "dp_1")
 DP_TILE = ("dp_0", "dp_1", "tile_0", "tile_1", "tile_2")
-
-
-def one_axis_at_a_time(value, axes):
-    return functools.reduce(lax.psum, axes, value)
 
 
 def row_tables(positions, length):
@@ -125,15 +120,12 @@
     back_local = products(local_weight, gate_grad, "co,sohw->schw")
     out_grad = to_owners(gate_grad, mode_scale)
     in_grad = mix_backward(out_grad, mode_weight).astype(jnp.bfloat16)
-    mode_term = weight_term(spectra, out_grad)
+    every_x = lax.all_gather(spectra, DP, axis=1, tiled=True)
+    every_g = lax.all_gather(out_grad, DP, axis=1, tiled=True)
+    mode_grad = weight_term(every_x, every_g)
     result = (to_pixels(in_grad, spec_scale) + back_local).astype(jnp.bfloat16)
-    groups = [(result, mode_term, local_term)]
-    input_grad = jnp.concatenate([group[0] for group in groups], axis=0)
-    mode_sum = groups[0][1]
-    local_sum = groups[0][2]
-    mode_grad = lax.psum(mode_sum.astype(jnp.bfloat16), DP).astype(jnp.float32)
-    local_grad = one_axis_at_a_time(local_sum, DP_TILE)
-    return (input_grad, mode_grad, local_grad)
+    local_grad = lax.psum(local_term, DP_TILE)
+    return (result, mode_grad, local_grad)
 
 
 def solution(mesh):

time: 238 us -> 254 us (1.067)
  the two profiles are of different devices: /device:TPU:8 before, /device:TPU:1 now
where the time goes in v1:
time: 254 us; the launch traced here: 249 us
  blocking collectives  91.2 us (36%)
  local copies, waits for them, and re-layouts  53.6 us (21%)
  starting transfers between devices  39.3 us (15%)
  waiting for transfers between devices  29.7 us (12%)
  matrix products  23.3 us (9%)
  other arithmetic  10.6 us (4%)
    psum x1, blocking collectives, local(): local_grad = lax.psum(local_term, DP_TILE)  77.5 us
    unnamed x58, local copies, waits for them, and re-layouts  30.4 us
    all_to_all x2, starting transfers between devices, to_owners(): lax.all_to_all(halves, TILE, split_axis=1, concat_axis=4, tiled=True)  23.6 us
    dot_general x21, matrix products, products(): return jnp.einsum(form, left, right, preferred_element_type=jnp.float32)  22.2 us
    all_to_all x2, waiting for transfers between devices, to_pixels(): lax.all_to_all(inner, TILE, split_axis=4, concat_axis=0, tiled=True)  21.7 us
    all_to_all x2, starting transfers between devices, to_pixels(): lax.all_to_all(inner, TILE, split_axis=4, concat_axis=0, tiled=True)  15.8 us
    reshape x4, local copies, waits for them, and re-layouts, to_owners(): halves = halves.reshape(2, M2, samples, C, TH)  8.78 us
    all_to_all x2, waiting for transfers between devices, to_owners(): lax.all_to_all(halves, TILE, split_axis=1, concat_axis=4, tiled=True)  8.01 us
  transfers between devices with their start and end apart: 4, of which 3 were waited for; matrix products, arithmetic and copies ran while one was open for 12% of the time, Pallas kernels for 0%

profile of v1, /device:TPU:1, one launch (start us, length us, event | category | flops | bytes accessed | tf_op | source)
XLA Modules:
  0.0 249.3 jit_solution(11928839196418062222)
XLA Ops:
  0.9 1.8 convolution_convert_fusion.3
  6.1 15.9 %all-to-all-start = ((bf16[64,2,2048]{2,1,0:T(2,128)(2,1)}), bf16[64,2,2048]{2,1,0:T(2,128)(2,1)}, u32[]{:S(2)}, u32[]{:S(2)}) async-start(bf16[64,2,2048]{2,1,0:T(2,128)(2,1)} %reshape.237), calls=%async_computation | async-start | bytes 1048576 | tf_op jit(solution)/shard_map/all_to_all | solution.py:105
  22.4 1.6 copy.145
  24.1 1.6 copy.146
  25.8 2.7 %fusion.55 = bf16[64,1024]{0,1:T(8,128)(2,1)} fusion(s32[64]{0:T(128)S(1)} %compare_select_fusion), kind=kLoop, calls=%fused_computation.83 | loop fusion | flops 1179648 | bytes 131328 | tf_op jit(solution)/shard_map/neg | solution.py:39
  28.4 3.0 %cosine_convert_fusion = (bf16[1024,64]{1,0:T(8,128)(2,1)S(1)}, bf16[64,1024]{0,1:T(8,128)(2,1)}, bf16[64,1024]{0,1:T(8,128)(2,1)}, bf16[1024,64]{1,0:T(8,128)(2,1)}) fusion(s32[64]{0:T(128)S(1)} %compare_select_fusion), kind=kLoop, calls=%fused_computation.62 | loop fusion | flops 1048576 | bytes 524544 | tf_op jit(solution)/shard_map/slice | solution.py:36
  31.4 8.0 %all-to-all-done = bf16[64,2,2048]{2,1,0:T(2,128)(2,1)} async-done(((bf16[64,2,2048]{2,1,0:T(2,128)(2,1)}), bf16[64,2,2048]{2,1,0:T(2,128)(2,1)}, u32[]{:S(2)}, u32[]{:S(2)}) %all-to-all-start) | async-done | bytes 524320 | tf_op jit(solution)/shard_map/all_to_all | solution.py:105
  39.4 2.3 reshape.238
  47.0 2.7 %copy.95 = bf16[1,2,64,2,1024]{2,3,1,0,4:T(2,128)(2,1)S(1)} copy(bf16[1,2,64,2,1024]{4,3,2,1,0:T(2,128)(2,1)} %reshape.217) | data formatting | bytes 1048576 | tf_op jit(solution)/shard_map/reshape | solution.py:111
  51.2 7.4 %all-to-all-start.1 = ((bf16[64,2,2048]{2,1,0:T(2,128)(2,1)}), bf16[64,2,2048]{2,1,0:T(2,128)(2,1)}, u32[]{:S(2)}, u32[]{:S(2)}) async-start(bf16[64,2,2048]{2,1,0:T(2,128)(2,1)} %reshape.239), calls=%async_computation.1 | async-start | bytes 1048576 | tf_op jit(solution)/shard_map/all_to_all | solution.py:112
  60.1 1.8 fusion.34
  61.9 13.5 %all-to-all-done.1 = bf16[64,2,2048]{2,1,0:T(2,128)(2,1)} async-done(((bf16[64,2,2048]{2,1,0:T(2,128)(2,1)}), bf16[64,2,2048]{2,1,0:T(2,128)(2,1)}, u32[]{:S(2)}, u32[]{:S(2)}) %all-to-all-start.1) | async-done | bytes 524320 | tf_op jit(solution)/shard_map/all_to_all | solution.py:112
  75.4 3.0 %reshape.240 = bf16[1024,1,2,2,64]{4,3,2,1,0:T(2,128)(2,1)S(1)} reshape(bf16[64,2,2048]{2,1,0:T(2,128)(2,1)} %all-to-all-done.1) | data formatting | bytes 1048576
  78.4 3.0 %copy.97 = bf16[1,2,64,2,64,16]{4,5,3,2,1,0:T(8,128)(2,1)} copy(bf16[1,2,64,2,64,16]{2,3,1,5,4,0:T(2,128)(2,1)S(1)} %bitcast.208) | data formatting | bytes 1048576 | tf_op jit(solution)/shard_map/all_to_all | solution.py:112
  81.4 4.2 %fusion.5 = bf16[2,64,16,256]{3,2,1,0:T(8,128)(2,1)S(1)} fusion(f32[2,16,256,64]{2,3,1,0:T(8,128)} %fusion.34, bf16[2,64,16,256]{3,2,1,0:T(8,128)(2,1)} %param.5, bf16[2,64,256,1,1]{2,1,0,4,3:T(8,128)(2,1)} %bitcast.213, bf16[1,2,64,2,64,16]{4,5,3,2,1,0:T(8,128)(2,1)} %copy.97), kind=kOutput, calls=%fused_computation.9 | convolution fusion | flops 141033472 | bytes 4784128 | tf_op jit(solution)/shard_map/qsoph,pqw->sohw/dot_general | solution.py:54
  87.0 3.2 %reshape.218 = bf16[2,64,2,64,16]{1,0,3,4,2:T(2,128)(2,1)} reshape(bf16[128,2,64,16]{0,2,3,1:T(8,128)(2,1)} %convolution_convert_fusion.2) | data formatting | bytes 1048576 | tf_op jit(solution)/shard_map/reshape | solution.py:104
  90.1 3.9 %copy.102 = bf16[2,64,2,64,16]{3,4,2,0,1:T(8,128)(2,1)} copy(bf16[2,64,2,64,16]{1,0,3,4,2:T(2,128)(2,1)} %reshape.218) | data formatting | bytes 1048576 | tf_op jit(solution)/shard_map/reshape | solution.py:104
  94.0 3.0 %reshape.241 = bf16[64,2,2048]{2,1,0:T(2,128)(2,1)} reshape(bf16[64,2,2,16,64]{4,3,2,1,0:T(8,128)(2,1)} %bitcast.209) | data formatting | bytes 1048576
  97.0 7.7 %all-to-all-start.2 = ((bf16[64,2,2048]{2,1,0:T(2,128)(2,1)}), bf16[64,2,2048]{2,1,0:T(2,128)(2,1)}, u32[]{:S(2)}, u32[]{:S(2)}) async-start(bf16[64,2,2048]{2,1,0:T(2,128)(2,1)} %reshape.241), calls=%async_computation.2 | async-start | bytes 1048576 | tf_op jit(solution)/shard_map/all_to_all | solution.py:105
  104.8 7.5 %all_gather.7 = bf16[1,8,64,128]{3,2,0,1:T(8,128)(2,1)S(1)} all-gather(bf16[1,2,64,128]{3,2,0,1:T(8,128)(2,1)S(1)} %fusion.92), channel_id=1, replica_groups=mesh['dp_0'=2,'dp_1'=2,'tile_0'=2,'tile_1'=4,'tile_2'=8] {'dp_0','dp_1'}, dimensions={1}, use_global_device_ids=true | all-gather | bytes 163840 | tf_op jit(solution)/shard_map/all_gather | solution.py:123
  114.1 1.7 copy.148
  115.8 1.8 convolution_bitcast_fusion
  117.6 77.5 %psum.7 = f32[64,64]{0,1:T(8,128)S(1)} all-reduce(f32[64,64]{0,1:T(8,128)} %convolution_bitcast_fusion), channel_id=1, replica_groups=mesh['dp_0'=2,'dp_1'=2,'tile_0'=2,'tile_1'=4,'tile_2'=8] {'dp_0','dp_1',..., use_global_device_ids=true, to_apply=%region_0.1 | all-reduce | flops 4096 | bytes 32768 | tf_op jit(solution)/shard_map/psum | solution.py:127
  195.8 1.9 fusion.31
  197.7 2.3 reshape.242
  205.8 6.2 %all_gather.6 = bf16[1,8,64,128]{3,2,0,1:T(8,128)(2,1)S(1)} all-gather(bf16[1,2,64,128]{3,2,0,1:T(8,128)(2,1)S(1)} %fusion.93), channel_id=1, replica_groups=mesh['dp_0'=2,'dp_1'=2,'tile_0'=2,'tile_1'=4,'tile_2'=8] {'dp_0','dp_1'}, dimensions={1}, use_global_device_ids=true | all-gather | bytes 163840 | tf_op jit(solution)/shard_map/all_gather | solution.py:124
  215.3 8.3 %all-to-all-start.3 = ((bf16[64,2,2048]{2,1,0:T(2,128)(2,1)}), bf16[64,2,2048]{2,1,0:T(2,128)(2,1)S(1)}, u32[]{:S(2)}, u32[]{:S(2)}) async-start(bf16[64,2,2048]{2,1,0:T(2,128)(2,1)} %reshape.243), calls=%async_computation.3 | async-start | bytes 1048576 | tf_op jit(solution)/shard_map/all_to_all | solution.py:112
  225.7 2.5 %pad_maximum_fusion = f32[1,64,64,128]{1,2,3,0:T(8,128)} fusion(f32[1,64,64,64]{1,2,3,0:T(8,128)S(1)} %subtract_bitcast_fusion, f32[1,64,64,64]{1,2,3,0:T(8,128)S(1)} %add_bitcast_fusion), kind=kLoop, calls=%fused_computation | loop fusion | flops 524288 | bytes 4194304 | tf_op jit(solution)/shard_map/concatenate | solution.py:81
  228.2 5.3 %copy.124 = f32[1,64,64,128]{3,2,1,0:T(8,128)} copy(f32[1,64,64,128]{1,2,3,0:T(8,128)} %pad_maximum_fusion) | data formatting | bytes 4194304
  233.5 8.2 %all-to-all-done.3 = bf16[64,2,2048]{2,1,0:T(2,128)(2,1)S(1)} async-done(((bf16[64,2,2048]{2,1,0:T(2,128)(2,1)}), bf16[64,2,2048]{2,1,0:T(2,128)(2,1)S(1)}, u32[]{:S(2)}, u32[]{:S(2)}) %all-to-all-start.3) | async-done | bytes 524320 | tf_op jit(solution)/shard_map/all_to_all | solution.py:112
  243.4 3.2 %copy.113 = bf16[1,2,64,2,64,16]{4,5,3,2,1,0:T(8,128)(2,1)S(1)} copy(bf16[1,2,64,2,64,16]{2,3,1,5,4,0:T(2,128)(2,1)} %bitcast.210) | data formatting | bytes 1048576 | tf_op jit(solution)/shard_map/all_to_all | solution.py:112
  246.6 2.4 fusion.6
  (97 shorter events, 28.8 us)
Async XLA Ops:
  0.6 59.5 %copy-start = (bf16[64,64]{1,0:T(8,128)(2,1)S(1)}, bf16[64,64]{1,0:T(8,128)(2,1)}, u32[]{:S(2)}) copy-start(bf16[64,64]{1,0:T(8,128)(2,1)} %param.7) | copy-start | bytes 24580
  0.9 1.8 copy-start.9
  0.9 1.8 copy-start.11
  3.1 18.8 %copy-start.3 = (bf16[1,64,64,128]{3,2,1,0:T(8,128)(2,1)S(1)}, bf16[1,64,64,128]{3,2,1,0:T(8,128)(2,1)}, u32[]{:S(2)}) copy-start(bf16[1,64,64,128]{3,2,1,0:T(8,128)(2,1)} %param.6) | copy-start | bytes 3145732
  6.1 33.3 %all-to-all-start = ((bf16[64,2,2048]{2,1,0:T(2,128)(2,1)}), bf16[64,2,2048]{2,1,0:T(2,128)(2,1)}, u32[]{:S(2)}, u32[]{:S(2)}) async-start(bf16[64,2,2048]{2,1,0:T(2,128)(2,1)} %reshape.237), calls=%async_computation | async-start | bytes 1048576 | tf_op jit(solution)/shard_map/all_to_all | solution.py:105
  25.7 18.7 %copy-start.4 = (bf16[1,64,64,64]{2,1,3,0:T(8,128)(2,1)}, bf16[1,64,64,64]{2,1,3,0:T(8,128)(2,1)S(1)}, u32[]{:S(2)}) copy-start(bf16[1,64,64,64]{2,1,3,0:T(8,128)(2,1)S(1)} %copy.146) | copy-start | bytes 1572868
  41.7 1.0 copy-start.6
  44.1 1.3 copy-start.14
  44.1 1.3 copy-start.16
  44.1 1.3 copy-start.18
  47.0 13.1 %copy-start.2 = (bf16[2,64,16,256]{3,2,1,0:T(8,128)(2,1)S(1)}, bf16[2,64,16,256]{3,2,1,0:T(8,128)(2,1)}, u32[]{:S(2)}) copy-start(bf16[2,64,16,256]{3,2,1,0:T(8,128)(2,1)} %param.4) | copy-start | bytes 3145732
  51.2 24.1 %all-to-all-start.1 = ((bf16[64,2,2048]{2,1,0:T(2,128)(2,1)}), bf16[64,2,2048]{2,1,0:T(2,128)(2,1)}, u32[]{:S(2)}, u32[]{:S(2)}) async-start(bf16[64,2,2048]{2,1,0:T(2,128)(2,1)} %reshape.239), calls=%async_computation.1 | async-start | bytes 1048576 | tf_op jit(solution)/shard_map/all_to_all | solution.py:112
  81.4 4.2 %copy-start.10 = (bf16[64,256]{1,0:T(8,128)(2,1)S(1)}, bf16[64,256]{1,0:T(8,128)(2,1)}, u32[]{:S(2)}) copy-start(bf16[64,256]{1,0:T(8,128)(2,1)} %copy-done.9) | copy-start | bytes 98308
  81.4 4.2 %copy-start.12 = (bf16[64,256]{1,0:T(8,128)(2,1)S(1)}, bf16[64,256]{1,0:T(8,128)(2,1)}, u32[]{:S(2)}) copy-start(bf16[64,256]{1,0:T(8,128)(2,1)} %copy-done.11) | copy-start | bytes 98308
  97.0 100.7 %all-to-all-start.2 = ((bf16[64,2,2048]{2,1,0:T(2,128)(2,1)}), bf16[64,2,2048]{2,1,0:T(2,128)(2,1)}, u32[]{:S(2)}, u32[]{:S(2)}) async-start(bf16[64,2,2048]{2,1,0:T(2,128)(2,1)} %reshape.241), calls=%async_computation.2 | async-start | bytes 1048576 | tf_op jit(solution)/shard_map/all_to_all | solution.py:105
  200.0 1.0 copy-start.7
  201.0 2.4 copy-start.5
  202.8 2.1 copy-start.15
  202.8 2.1 copy-start.17
  202.8 2.1 copy-start.19
  212.8 10.8 %copy-start.8 = (bf16[1,8,64,64]{2,1,3,0:T(8,128)(2,1)S(1)}, bf16[1,8,64,64]{2,1,3,0:T(8,128)(2,1)}, u32[]{:S(2)}) copy-start(bf16[1,8,64,64]{2,1,3,0:T(8,128)(2,1)} %copy.148) | copy-start | bytes 196612
  215.3 8.9 %copy-start.13 = (bf16[1,8,64,64]{3,2,0,1:T(8,128)(2,1)S(1)}, bf16[1,8,64,64]{3,2,0,1:T(8,128)(2,1)}, u32[]{:S(2)}) copy-start(bf16[1,8,64,64]{3,2,0,1:T(8,128)(2,1)} %get-tuple-element.14) | copy-start | bytes 196612
  215.3 26.5 %all-to-all-start.3 = ((bf16[64,2,2048]{2,1,0:T(2,128)(2,1)}), bf16[64,2,2048]{2,1,0:T(2,128)(2,1)S(1)}, u32[]{:S(2)}, u32[]{:S(2)}) async-start(bf16[64,2,2048]{2,1,0:T(2,128)(2,1)} %reshape.243), calls=%async_computation.3 | async-start | bytes 1048576 | tf_op jit(solution)/shard_map/all_to_all | solution.py:112
  233.5 13.1 %copy-start.1 = (f32[2,16,256,64]{2,3,1,0:T(8,128)S(1)}, f32[2,16,256,64]{2,3,1,0:T(8,128)}, u32[]{:S(2)}) copy-start(f32[2,16,256,64]{2,3,1,0:T(8,128)} %fusion.31) | copy-start | bytes 6291460
  233.5 13.1 %copy-start.20 = (bf16[128,256]{1,0:T(8,128)(2,1)S(1)}, bf16[128,256]{1,0:T(8,128)(2,1)}, u32[]{:S(2)}) copy-start(bf16[128,256]{1,0:T(8,128)(2,1)} %maximum_convert_fusion) | copy-start | bytes 196612

commit v2 on v1

v2 whole, which is shorter than its diff:
```python
import math

import jax
import jax.numpy as jnp
import numpy as np
from jax import lax
from jax.experimental import pallas as pl
from jax.experimental.pallas import tpu as pltpu
from jax.sharding import PartitionSpec as P

C = 64
M1 = 64
M2 = 64
W = 256
TH = 16
H = 1024
N_TILE = 64
N_DP = 4
S = 2
RH = 8
RL = 2
SPEC = 1.0 / math.sqrt(H * W)
MODE = 1.0 / math.sqrt(M1 * M2)
F32 = jnp.float32
BF16 = jnp.bfloat16
MESH = pl.DeviceIdType.MESH


def column_rows():
    phase = np.mod(np.arange(M2)[:, None] * np.arange(W)[None, :], W) * (2.0 * math.pi / W)
    return np.stack([np.cos(phase), -np.sin(phase)], axis=1).reshape(2 * M2, W)


def row_maps():
    modes = np.arange(M1)
    signed = np.where(modes < M1 // 2, modes, modes - M1)
    phase = np.mod(np.arange(H)[:, None] * signed[None, :], H) * (2.0 * math.pi / H)
    cosine = np.cos(phase).reshape(N_TILE, RH, RL, M1)
    sine = np.sin(phase).reshape(N_TILE, RH, RL, M1)
    first = np.concatenate([cosine, -sine], axis=-1)
    second = np.concatenate([sine, cosine], axis=-1)
    return np.stack([first, second], axis=1).reshape(N_TILE * 2 * RH, RL * 2 * M1)


def mm(left, right):
    return lax.dot_general(left, right, (((1,), (0,)), ((), ())), preferred_element_type=F32)


def mm_nt(left, right):
    return lax.dot_general(left, right, (((1,), (1,)), ((), ())), preferred_element_type=F32)


def gelu_slope(values):
    cumulative = 0.5 * (1.0 + lax.erf(values * (1.0 / math.sqrt(2.0))))
    density = jnp.exp(-0.5 * values * values) * (1.0 / math.sqrt(2.0 * math.pi))
    return cumulative + values * density


def kernel(v_hbm, ct_hbm, w_hbm, mix_hbm, col_hbm, inv_hbm, fwd_hbm,
           og_hbm, mg_hbm, lg_hbm,
           v, ct, w16, w32, wt32, mix, col, inv, fwd, m32, b32, gg, og, snd, rcv,
           xs, ds, xall, dall, pa, pb, x1, x2, d1, d2, mg, lga, lgs, lg1, lgr, lgp, lgd, lge, lgf,
           load_sem, send_sem, recv_sem, dp_send, dp_recv, lg_send, lg_recv, out_sem):
    me = lax.axis_index("tile")
    my = lax.axis_index("dp")
    me_y, me_x, me_z = lax.div(me, 32), lax.rem(lax.div(me, 8), 4), lax.rem(me, 8)

    def partner(i):
        j, k = lax.div(i, 8), lax.rem(i, 8)
        kx = lax.rem(k, 4)
        dz = 4 + (1 - 2 * lax.rem(j, 2)) * lax.div(j + 1, 2)
        dx = 2 + (1 - 2 * lax.rem(kx, 2)) * lax.div(kx + 1, 2)
        dy = 1 - lax.div(k, 4)
        return lax.rem(me_y + dy, 2) * 32 + lax.rem(me_x + dx, 4) * 8 + lax.rem(me_z + dz, 8)

    def group(j):
        return lax.rem(my + j, N_DP)

    loads = [
        pltpu.make_async_copy(a, b, load_sem.at[n])
        for n, (a, b) in enumerate([
            (col_hbm, col), (v_hbm.at[0], v.at[0]), (v_hbm.at[1], v.at[1]), (fwd_hbm, fwd),
            (w_hbm, w16), (inv_hbm, inv), (mix_hbm, mix), (ct_hbm, ct)])
    ]
    for copy in loads:
        copy.start()

    barrier = pltpu.get_barrier_semaphore()

    def greet(i, carry):
        pl.semaphore_signal(barrier, inc=1, device_id={"tile": partner(i)}, device_id_type=MESH)
        return carry

    lax.fori_loop(0, N_TILE - 1, greet, 0)
    for j in range(1, N_DP):
        pl.semaphore_signal(barrier, inc=1, device_id={"dp": group(j)}, device_id_type=MESH)

    lane = lax.broadcasted_iota(jnp.int32, (C, 128), 1)
    low = lane < 64
    sgn = jnp.where(low, 1.0, -1.0).astype(F32)

    def exchange(phase, s):
        def send(i, carry):
            p = partner(i)
            pltpu.make_async_remote_copy(
                src_ref=snd.at[phase, s, pl.ds(pl.multiple_of(p * 16, 16), 16), :],
                dst_ref=rcv.at[phase, s, pl.ds(pl.multiple_of(me * 16, 16), 16), :],
                send_sem=send_sem.at[phase, s], recv_sem=recv_sem.at[phase, s],
                device_id={"tile": p}, device_id_type=MESH).start()
            return carry

        lax.fori_loop(0, N_TILE - 1, send, 0)
        mine = pl.ds(pl.multiple_of(me * 16, 16), 16)
        pltpu.make_async_copy(
            snd.at[phase, s, mine, :], rcv.at[phase, s, mine, :], recv_sem.at[phase, s]).start()

    def arrived(phase, s):
        pltpu.make_async_copy(rcv.at[phase, s], rcv.at[phase, s], recv_sem.at[phase, s]).wait()

    def to_group(src, dst, s, n):
        for j in range(1, N_DP):
            pltpu.make_async_remote_copy(
                src_ref=src.at[s], dst_ref=dst.at[my, s], send_sem=dp_send.at[n], recv_sem=dp_recv.at[n],
                device_id={"dp": group(j)}, device_id_type=MESH).start()
        pltpu.make_async_copy(src.at[s], dst.at[my, s], dp_recv.at[n]).start()

    def pack(phase, s):
        snd[phase, s] = m32[...].astype(BF16)

    loads[0].wait()
    for s in range(S):
        loads[1 + s].wait()

        def column(r, carry):
            tile = v[s, pl.ds(pl.multiple_of(r * 128, 128), 128), :]
            m32[pl.ds(r, 128, stride=RH), :] = mm_nt(col[...], tile)
            return carry

        lax.fori_loop(0, RH, column, 0)
        pack(0, s)
        if s == 0:
            pl.semaphore_wait(barrier, N_TILE - 1 + N_DP - 1)
        exchange(0, s)

    loads[4].wait()

    def widen(c, carry):
        at = pl.ds(pl.multiple_of(c * 64, 64), 64)
        w32[at, :] = w16[at, :].astype(F32)
        return carry

    lax.fori_loop(0, C, widen, 0)

    def spectrum(phase, s, scale):
        both = mm(fwd[...], rcv[phase, s])
        turned = (both[:128] + pltpu.roll(both[128:], 64, 1)).T
        return (turned[:64] * scale).astype(BF16)

    def halves(value):
        wide = value.astype(F32)
        other = pltpu.roll(wide, 64, 1)
        pa[...] = jnp.where(low, wide, other)
        pb[...] = jnp.where(low, other, wide)

    def mix_rows(table):
        def step(c, carry):
            first, second = carry
            block = table[pl.ds(pl.multiple_of(c * 64, 64), 64), :]
            return first + pa[pl.ds(c, 1), :] * block, second + pb[pl.ds(c, 1), :] * block

        zero = jnp.zeros((C, 128), F32)
        return lax.fori_loop(0, C, step, (zero, zero), unroll=4)

    def back_to_rows(phase, s, value, scale):
        small = (value.astype(BF16).astype(F32) * scale).astype(BF16)
        none = jnp.zeros_like(small)
        right = jnp.concatenate(
            [jnp.concatenate([small, none], axis=1), jnp.concatenate([none, small], axis=1)], axis=0)

        def rows(n, carry):
            at = pl.ds(pl.multiple_of(n * 256, 256), 256)
            snd[phase, s, at, :] = mm_nt(inv[at, :], right).astype(BF16)
            return carry

        lax.fori_loop(0, 4, rows, 0)
        exchange(phase, s)

    loads[3].wait()
    loads[5].wait()
    for s in range(S):
        arrived(0, s)
        xs[s] = spectrum(0, s, SPEC)
        to_group(xs, xall, s, 0)
        halves(xs[s])
        first, second = mix_rows(w32)
        back_to_rows(1, s, first - sgn * pltpu.roll(second, 64, 1), MODE)

    def swap(o, carry):
        wt32[pl.ds(pl.multiple_of(o * 64, 64), 64), :] = w32[pl.ds(o, 64, stride=64), :]
        return carry

    lax.fori_loop(0, C, swap, 0)
    loads[6].wait()
    loads[7].wait()
    lga[...] = jnp.zeros_like(lga)

    for s in range(S):
        arrived(1, s)
        b32[...] = rcv[1, s].astype(F32)

        def gate(r, carry):
            at = pl.ds(pl.multiple_of(r * 128, 128), 128)
            spectral = b32[pl.ds(r, 128, stride=RH), :].T.astype(BF16)
            tile = v[s, at, :]
            pre = mm(spectral, col[...]) + mm(mix[0], tile)
            grad = (ct[s, at, :].astype(F32) * gelu_slope(pre)).astype(BF16)
            gg[s, at, :] = grad
            m32[pl.ds(r, 128, stride=RH), :] = mm_nt(col[...], grad)
            lga[...] += mm_nt(tile, grad)
            return carry

        lax.fori_loop(0, RH, gate, 0)
        pack(2, s)
        exchange(2, s)

    lgs[...] = lga[:64] + pltpu.roll(lga[64:], 64, 1)

    def spread(c, carry):
        lg1[c] = lgs[pl.ds(c, 1), :]
        return carry

    lax.fori_loop(0, C, spread, 0)

    def send_rows(src_of, dst, n):
        def send(i, carry):
            p = partner(i)
            pltpu.make_async_remote_copy(
                src_ref=src_of(p), dst_ref=dst.at[me], send_sem=lg_send.at[n], recv_sem=lg_recv.at[n],
                device_id={"tile": p}, device_id_type=MESH).start()
            return carry

        lax.fori_loop(0, N_TILE - 1, send, 0)
        pltpu.make_async_copy(src_of(me), dst.at[me], lg_recv.at[n]).start()

    send_rows(lambda p: lg1.at[p], lgr, 0)

    for s in range(S):
        arrived(2, s)
        ds[s] = spectrum(2, s, MODE)
        to_group(ds, dall, s, 1)
        halves(ds[s])
        first, second = mix_rows(wt32)
        back_to_rows(3, s, pltpu.roll(second, 64, 1) + sgn * first, SPEC)

    pltpu.make_async_copy(lgr, lgr, lg_recv.at[0]).wait()
    lgp[0] = jnp.sum(lgr[...], axis=0)
    for j in range(1, N_DP):
        pltpu.make_async_remote_copy(
            src_ref=lgp.at[0], dst_ref=lgd.at[my], send_sem=lg_send.at[2], recv_sem=lg_recv.at[2],
            device_id={"dp": group(j)}, device_id_type=MESH).start()
    pltpu.make_async_copy(lgp.at[0], lgd.at[my], lg_recv.at[2]).start()

    pltpu.make_async_copy(xall, xall, dp_recv.at[0]).wait()
    pltpu.make_async_copy(dall, dall, dp_recv.at[1]).wait()
    for g in range(N_DP):
        for s in range(S):
            n = g * S + s
            wide = xall[g, s].astype(F32)
            other = pltpu.roll(wide, 64, 1)
            x1[n] = jnp.where(low, wide, other)
            x2[n] = jnp.where(low, other, -wide)
            grad = dall[g, s].astype(F32)
            d1[n] = grad
            d2[n] = pltpu.roll(grad, 64, 1)

    pltpu.make_async_copy(lgd, lgd, lg_recv.at[2]).wait()
    lge[0] = jnp.sum(lgd[...], axis=0)
    send_rows(lambda p: lge.at[0], lgf, 1)

    def outer(c, carry):
        even = jnp.zeros((C, 128), F32)
        odd = jnp.zeros((C, 128), F32)
        for n in range(N_DP * S):
            first, second = d1[n], d2[n]
            even += x1[n, pl.ds(2 * c, 1), :] * first + x2[n, pl.ds(2 * c, 1), :] * second
            odd += x1[n, pl.ds(2 * c + 1, 1), :] * first + x2[n, pl.ds(2 * c + 1, 1), :] * second
        at = pl.multiple_of(c * 128, 128)
        mg[pl.ds(at, 64), :] = even
        mg[pl.ds(at + 64, 64), :] = odd
        pltpu.make_async_copy(mg.at[pl.ds(at, 128), :], mg_hbm.at[pl.ds(at, 128), :], out_sem.at[0]).start()
        return carry

    lax.fori_loop(0, C // 2, outer, 0)

    for s in range(S):
        arrived(3, s)
        b32[...] = rcv[3, s].astype(F32)

        def back(r, carry):
            at = pl.ds(pl.multiple_of(r * 128, 128), 128)
            spectral = b32[pl.ds(r, 128, stride=RH), :].T.astype(BF16)
            og[s, at, :] = (mm(spectral, col[...]) + mm(mix[1], gg[s, at, :])).astype(BF16)
            pltpu.make_async_copy(og.at[s, at, :], og_hbm.at[s, at, :], out_sem.at[1]).start()
            return carry

        lax.fori_loop(0, RH, back, 0)

    pltpu.make_async_copy(lgf, lgf, lg_recv.at[1]).wait()
    tail = pltpu.make_async_copy(lgf, lg_hbm, out_sem.at[2])
    tail.start()

    for phase in range(4):
        for s in range(S):
            sent = snd.at[phase, s, pl.ds(0, 16 * (N_TILE - 1)), :]
            pltpu.make_async_copy(sent, sent, send_sem.at[phase, s]).wait()
    for n, ref in ((0, xall), (1, dall)):
        sent = ref.at[pl.ds(0, N_DP - 1)]
        pltpu.make_async_copy(sent, sent, dp_send.at[n]).wait()
    for n in range(2):
        sent = lgr.at[pl.ds(0, N_TILE - 1)]
        pltpu.make_async_copy(sent, sent, lg_send.at[n]).wait()
    sent = lgd.at[pl.ds(0, N_DP - 1)]
    pltpu.make_async_copy(sent, sent, lg_send.at[2]).wait()
    pltpu.make_async_copy(mg, mg_hbm, out_sem.at[0]).wait()
    pltpu.make_async_copy(og, og_hbm, out_sem.at[1]).wait()
    tail.wait()


def step(inputs, cotangent, mode_weight, local_weight):
    def row_major(field):
        return jnp.swapaxes(field, 1, 2).reshape(S, TH * C, W)

    paired = jnp.tile(local_weight, (2, 2))
    same = jnp.asarray(np.kron(np.eye(2), np.ones((C, C))).astype(bool))
    mixes = jnp.where(same[None], jnp.stack([paired.T, paired]), jnp.zeros((), BF16))
    rows = row_maps()
    col = jnp.asarray(column_rows(), BF16)
    inv = jnp.asarray(rows, BF16)
    fwd = jnp.asarray(np.ascontiguousarray(rows.T), BF16)
    dma = pltpu.SemaphoreType.DMA
    vm = pltpu.VMEM
    og, mg, lg = pl.pallas_call(
        kernel,
        out_shape=(
            jax.ShapeDtypeStruct((S, TH * C, W), BF16),
            jax.ShapeDtypeStruct((C * C, 2 * M1), F32),
            jax.ShapeDtypeStruct((C, 1, 128), F32),
        ),
        in_specs=[pl.BlockSpec(memory_space=pl.ANY)] * 7,
        out_specs=(pl.BlockSpec(memory_space=pl.ANY),) * 3,
        scratch_shapes=[
            vm((S, TH * C, W), BF16), vm((S, TH * C, W), BF16),
            vm((C * C, 128), BF16), vm((C * C, 128), F32), vm((C * C, 128), F32),
            vm((2, 128, 128), BF16), vm((128, W), BF16), vm((1024, 256), BF16), vm((256, 1024), BF16),
            vm((1024, 128), F32), vm((1024, 128), F32),
            vm((S, TH * C, W), BF16), vm((S, TH * C, W), BF16),
            vm((4, S, 1024, 128), BF16), vm((4, S, 1024, 128), BF16),
            vm((S, C, 128), BF16), vm((S, C, 128), BF16),
            vm((N_DP, S, C, 128), BF16), vm((N_DP, S, C, 128), BF16),
            vm((C, 128), F32), vm((C, 128), F32),
            vm((N_DP * S, C, 128), F32), vm((N_DP * S, C, 128), F32),
            vm((N_DP * S, C, 128), F32), vm((N_DP * S, C, 128), F32),
            vm((C * C, 128), F32),
            vm((128, 128), F32), vm((C, 128), F32),
            vm((C, 1, 128), F32), vm((C, 1, 128), F32), vm((1, 1, 128), F32), vm((N_DP, 1, 128), F32),
            vm((1, 1, 128), F32), vm((C, 1, 128), F32),
            dma((8,)), dma((4, S)), dma((4, S)), dma((2,)), dma((2,)), dma((3,)), dma((3,)), dma((3,)),
        ],
        compiler_params=pltpu.CompilerParams(
            collective_id=0, has_side_effects=True, vmem_limit_bytes=48 << 20),
    )(row_major(inputs), row_major(cotangent), mode_weight.reshape(C * C, 2 * M1), mixes, col, inv, fwd)
    input_grad = jnp.swapaxes(og.reshape(S, TH, C, W), 1, 2)
    return input_grad, mg.reshape(1, C, C, 2 * M1), lg[:, 0, :C]


def solution(mesh):
    in_specs = (P("dp", None, "tile", None), P("dp", None, "tile", None), P("tile", None, None, None), P())
    out_specs = (P("dp", None, "tile", None), P("tile", None, None, None), P())
    return jax.shard_map(step, mesh=mesh, in_specs=in_specs, out_specs=out_specs, check_vma=False)
```

time: 254 us -> 77.9 us (0.31); the launches traced: 249 us -> 77.7 us
  blocking collectives: 91.2 us -> 0 us
  Pallas kernels: 0 us -> 69.4 us
  local copies, waits for them, and re-layouts: 53.6 us -> 6.8 us
  starting transfers between devices: 39.3 us -> 0 us
  waiting for transfers between devices: 29.7 us -> 0 us
  matrix products: 23.3 us -> 0 us
  other arithmetic: 10.6 us -> 0.74 us
    psum x1 -> x0, blocking collectives: 77.5 us -> none  [local(): local_grad = lax.psum(local_term, DP_TILE)]
    pallas_call x0 -> x1, Pallas kernels: none -> 69.4 us  [step(): pl.pallas_call(kernel, out_shape=(jax.ShapeDtypeStruct((S, TH * C, W), BF...]
    all_to_all x4 -> x0, starting transfers between devices: 39.3 us -> none  [the longest x2 23.6 us: to_owners(): lax.all_to_all(halves, TILE, split_axis=1, concat_axis=4, tiled=True)]
    all_to_all x4 -> x0, waiting for transfers between devices: 29.7 us -> none  [the longest x2 21.7 us: to_pixels(): lax.all_to_all(inner, TILE, split_axis=4, concat_axis=0, tiled=True)]
    unnamed x58 -> x14, local copies, waits for them, and re-layouts: 30.4 us -> 2.04 us
    dot_general x23 -> x0, matrix products: 23.3 us -> none  [the longest x21 22.2 us: products(): return jnp.einsum(form, left, right, preferred_element_type=jnp.float32)]
    all_gather x2 -> x0, blocking collectives: 13.7 us -> none  [the longest x1 7.54 us: local(): every_x = lax.all_gather(spectra, DP, axis=1, tiled=True)]
    reshape x8 -> x1, local copies, waits for them, and re-layouts: 13.9 us -> 1.55 us  [step(): input_grad = jnp.swapaxes(og.reshape(S, TH, C, W), 1, 2)]
  transfers between devices with their start and end apart: 4 -> 0, of which waited for: 3 -> 0; matrix products, arithmetic and copies ran while one was open for 12% -> 0% of each run, Pallas kernels for 0% -> 0%
where the time goes in v2:
time: 77.9 us; the launch traced here: 77.7 us
  Pallas kernels  69.4 us (89%)
  local copies, waits for them, and re-layouts  6.8 us (9%)
    pallas_call x1, Pallas kernels, step(): pl.pallas_call(kernel, out_shape=(jax.ShapeDtypeStruct((S, TH * C, W), BF...  69.4 us
    transpose x2, local copies, waits for them, and re-layouts, row_major(): return jnp.swapaxes(field, 1, 2).reshape(S, TH * C, W)  2.06 us
    unnamed x14, local copies, waits for them, and re-layouts  2.04 us

profile of v2, /device:TPU:1, one launch (start us, length us, event | category | flops | bytes accessed | tf_op | source)
XLA Modules:
  0.0 77.7 jit_solution(16533146895769260288)
XLA Ops:
  0.6 0.0 copy-start.5
  0.6 0.8 %tile.4 = bf16[2,64,2,64]{3,2,1,0:T(2,128)(2,1)S(1)} broadcast(bf16[64,64]{1,0:T(8,128)(2,1)} %param.11), dimensions={1,3} | broadcast | bytes 40960 | tf_op jit(solution)/shard_map/tile | solution.py:333
  1.5 0.1 stack_tile.3
  1.6 0.1 reshape.28
  1.7 0.1 copy.15
  1.8 0.7 maximum_select_fusion.mix_hbm
  2.5 0.0 copy-start
  2.6 0.0 copy-start.1
  2.6 0.0 copy-start.2
  2.6 0.0 copy-start.3
  2.6 1.7 %copy.11 = bf16[2,16,64,256]{3,2,1,0:T(8,128)(2,1)S(1)} copy(bf16[2,16,64,256]{3,1,2,0:T(8,128)(2,1)} %bitcast.22) | data formatting | bytes 2097152 | tf_op jit(solution)/shard_map/transpose | solution.py:331
  4.3 0.0 copy-done.5
  4.3 0.3 copy.12
  4.7 0.0 copy-done
  4.7 0.0 copy-done.1
  4.7 0.0 copy-done.2
  4.7 0.0 copy-done.3
  4.7 69.4 %shard_map.103 = (bf16[2,1024,256]{2,1,0:T(8,128)(2,1)S(1)}, f32[4096,128]{1,0:T(8,128)}, f32[64,1,128]{2,1,0:T(1,128)S(1)}) custom-call(bf16[2,1024,256]{2,1,0:T(8,128)(2,1)S(1)} %bitcast.16, bf16[2,1024,256]{2,1,0:T(8,128)(2,1)S(1)} %bitcast.17, bf16[4096,128]{1,0:T(8,128)(2,1)S(1)} %bitcast.19, bf16[2,128,128]{2,1,0:T(8,128)(2,1)S(1)} %maximum_select_fusion.mix_hbm, ...), custom_call_target="tpu_custom_call" | custom-call | tf_op jit(solution)/shard_map/pallas_call | solution.py:342
  74.1 0.0 copy-start.4
  74.1 1.6 %copy.17 = bf16[2,16,64,256]{3,1,2,0:T(8,128)(2,1)} copy(bf16[2,16,64,256]{3,2,1,0:T(8,128)(2,1)S(1)} %bitcast.18) | data formatting | bytes 2097152 | tf_op jit(solution)/shard_map/reshape | solution.py:372
  75.6 0.1 copy-done.4
  75.7 1.3 %copy.20 = f32[1,64,64,128]{3,2,1,0:T(8,128)} copy(f32[1,64,64,128]{3,2,1,0:T(8,128)S(1)} %bitcast.21) | data formatting | bytes 4194304
  77.0 0.6 copy.21
Async XLA Ops:
  0.6 3.7 %copy-start.5 = (bf16[2,64,16,256]{3,2,1,0:T(8,128)(2,1)S(1)}, bf16[2,64,16,256]{3,2,1,0:T(8,128)(2,1)}, u32[]{:S(2)}) copy-start(bf16[2,64,16,256]{3,2,1,0:T(8,128)(2,1)} %param.9) | copy-start | bytes 3145732
  2.5 2.1 %copy-start = (bf16[1,64,64,128]{3,2,1,0:T(8,128)(2,1)S(1)}, bf16[1,64,64,128]{3,2,1,0:T(8,128)(2,1)}, u32[]{:S(2)}) copy-start(bf16[1,64,64,128]{3,2,1,0:T(8,128)(2,1)} %param.10) | copy-start | bytes 3145732
  2.6 2.1 %copy-start.1 = (bf16[256,1024]{1,0:T(8,128)(2,1)S(1)}, bf16[256,1024]{1,0:T(8,128)(2,1)}, u32[]{:S(2)}) copy-start(bf16[256,1024]{1,0:T(8,128)(2,1)} %constant.13.clone.fwd_hbm) | copy-start | bytes 1572868
  2.6 2.1 %copy-start.2 = (bf16[1024,256]{1,0:T(8,128)(2,1)S(1)}, bf16[1024,256]{1,0:T(8,128)(2,1)}, u32[]{:S(2)}) copy-start(bf16[1024,256]{1,0:T(8,128)(2,1)} %constant.12.clone.inv_hbm) | copy-start | bytes 1572868
  2.6 2.1 %copy-start.3 = (bf16[128,256]{1,0:T(8,128)(2,1)S(1)}, bf16[128,256]{1,0:T(8,128)(2,1)}, u32[]{:S(2)}) copy-start(bf16[128,256]{1,0:T(8,128)(2,1)} %constant.11.clone.col_hbm) | copy-start | bytes 196612
  74.1 1.6 %copy-start.4 = (f32[4096,128]{1,0:T(8,128)S(1)}, f32[4096,128]{1,0:T(8,128)}, u32[]{:S(2)}) copy-start(f32[4096,128]{1,0:T(8,128)} %get-tuple-element.7) | copy-start | bytes 6291460

commit v3 on v2

--- a/solution.py
+++ b/solution.py
@@ -19,6 +19,7 @@
 S = 2
 RH = 8
 RL = 2
+FAR_FIRST = (4, 3, 5, 2, 6, 1, 7, 0)
 SPEC = 1.0 / math.sqrt(H * W)
 MODE = 1.0 / math.sqrt(M1 * M2)
 F32 = jnp.float32
@@ -56,22 +57,62 @@
     return cumulative + values * density
 
 
-def kernel(v_hbm, ct_hbm, w_hbm, mix_hbm, col_hbm, inv_hbm, fwd_hbm,
-           og_hbm, mg_hbm, lg_hbm,
-           v, ct, w16, w32, wt32, mix, col, inv, fwd, m32, b32, gg, og, snd, rcv,
-           xs, ds, xall, dall, pa, pb, x1, x2, d1, d2, mg, lga, lgs, lg1, lgr, lgp, lgd, lge, lgf,
-           load_sem, send_sem, recv_sem, dp_send, dp_recv, lg_send, lg_recv, out_sem):
+def input_gradient(received, grad, mix, col, b32, wide, result):
+    b32[...] = received[...].astype(F32)
+
+    def back(r, carry):
+        spectral = b32[pl.ds(r, 128, stride=RH), :].T.astype(BF16)
+        value = mm(spectral, col[...]) + mm(mix[...], grad[pl.ds(pl.multiple_of(r * 128, 128), 128), :])
+        for n in range(RL):
+            for half in range(2):
+                wide[half, pl.ds(2 * r + n, C, stride=TH), :] = value[n * C:(n + 1) * C, half * 128:(half + 1) * 128]
+        return carry
+
+    lax.fori_loop(0, RH, back, 0, unroll=2)
+    for half in range(2):
+        result[:, half * 128:(half + 1) * 128] = wide[half].astype(BF16)
+
+
+def finish(og0, mg, lg, last, ggl, mixl, coll, og_hbm, mg_hbm, lg_hbm, b32, wide, og1, sem):
+    copies = [
+        pltpu.make_async_copy(a, b, sem.at[n])
+        for n, (a, b) in enumerate([(mg, mg_hbm), (og0, og_hbm.at[0]), (lg, lg_hbm), (og1, og_hbm.at[1])])
+    ]
+    for copy in copies[:3]:
+        copy.start()
+    input_gradient(last, ggl, mixl, coll, b32, wide, og1)
+    copies[3].start()
+    for copy in copies:
+        copy.wait()
+
+
+def kernel(v_hbm, ct_hbm, w_hbm, l_hbm, col_hbm, inv_hbm, fwd_hbm,
+           og, mg, lg, last, ggl, mixl, coll,
+           v, vn, v32, ctn, ct, w16, w32, wt32, l16, mix, col, inv, fwd, m32, b32, gg, snd, rcv,
+           xs, ds, xall, dall, pa, pb, x1, x2, d1, d2, lga, lgs, lg1, lgr, lgp, lgd, lge, lgf,
+           load_sem, send_sem, recv_sem, dp_send, dp_recv, lg_send, lg_recv):
     me = lax.axis_index("tile")
     my = lax.axis_index("dp")
     me_y, me_x, me_z = lax.div(me, 32), lax.rem(lax.div(me, 8), 4), lax.rem(me, 8)
 
-    def partner(i):
-        j, k = lax.div(i, 8), lax.rem(i, 8)
+    column_of = [lax.rem(me_z + dz, 8) for dz in range(8)]
+
+    def plane(k):
         kx = lax.rem(k, 4)
-        dz = 4 + (1 - 2 * lax.rem(j, 2)) * lax.div(j + 1, 2)
         dx = 2 + (1 - 2 * lax.rem(kx, 2)) * lax.div(kx + 1, 2)
         dy = 1 - lax.div(k, 4)
-        return lax.rem(me_y + dy, 2) * 32 + lax.rem(me_x + dx, 4) * 8 + lax.rem(me_z + dz, 8)
+        return lax.rem(me_y + dy, 2) * 32 + lax.rem(me_x + dx, 4) * 8
+
+    def to_others(send):
+        def planes(k, carry):
+            base = plane(k)
+            for dz in FAR_FIRST:
+                send(base + column_of[dz])
+            return carry
+
+        lax.fori_loop(0, 7, planes, 0)
+        for dz in FAR_FIRST[:-1]:
+            send(me_y * 32 + me_x * 8 + column_of[dz])
 
     def group(j):
         return lax.rem(my + j, N_DP)
@@ -79,19 +120,18 @@
     loads = [
         pltpu.make_async_copy(a, b, load_sem.at[n])
         for n, (a, b) in enumerate([
-            (col_hbm, col), (v_hbm.at[0], v.at[0]), (v_hbm.at[1], v.at[1]), (fwd_hbm, fwd),
-            (w_hbm, w16), (inv_hbm, inv), (mix_hbm, mix), (ct_hbm, ct)])
+            (col_hbm, col), (v_hbm.at[0], vn.at[0]), (v_hbm.at[1], vn.at[1]), (fwd_hbm, fwd),
+            (w_hbm, w16), (inv_hbm, inv), (l_hbm, l16), (ct_hbm, ctn)])
     ]
     for copy in loads:
         copy.start()
 
     barrier = pltpu.get_barrier_semaphore()
 
-    def greet(i, carry):
-        pl.semaphore_signal(barrier, inc=1, device_id={"tile": partner(i)}, device_id_type=MESH)
-        return carry
-
-    lax.fori_loop(0, N_TILE - 1, greet, 0)
+    def greet(p):
+        pl.semaphore_signal(barrier, inc=1, device_id={"tile": p}, device_id_type=MESH)
+
+    to_others(greet)
     for j in range(1, N_DP):
         pl.semaphore_signal(barrier, inc=1, device_id={"dp": group(j)}, device_id_type=MESH)
 
@@ -100,16 +140,14 @@
     sgn = jnp.where(low, 1.0, -1.0).astype(F32)
 
     def exchange(phase, s):
-        def send(i, carry):
-            p = partner(i)
+        def send(p):
             pltpu.make_async_remote_copy(
                 src_ref=snd.at[phase, s, pl.ds(pl.multiple_of(p * 16, 16), 16), :],
                 dst_ref=rcv.at[phase, s, pl.ds(pl.multiple_of(me * 16, 16), 16), :],
                 send_sem=send_sem.at[phase, s], recv_sem=recv_sem.at[phase, s],
                 device_id={"tile": p}, device_id_type=MESH).start()
-            return carry
-
-        lax.fori_loop(0, N_TILE - 1, send, 0)
+
+        to_others(send)
         mine = pl.ds(pl.multiple_of(me * 16, 16), 16)
         pltpu.make_async_copy(
             snd.at[phase, s, mine, :], rcv.at[phase, s, mine, :], recv_sem.at[phase, s]).start()
@@ -127,16 +165,27 @@
     def pack(phase, s):
         snd[phase, s] = m32[...].astype(BF16)
 
+    def rows_of(natural, r):
+        return jnp.concatenate([
+            jnp.concatenate([natural[half, pl.ds(2 * r + n, C, stride=TH), :] for half in range(2)], axis=1)
+            for n in range(RL)], axis=0)
+
+    def widen_into(natural, source):
+        for half in range(2):
+            natural[half] = source[:, half * 128:(half + 1) * 128].astype(F32)
+
     loads[0].wait()
     for s in range(S):
         loads[1 + s].wait()
 
         def column(r, carry):
-            tile = v[s, pl.ds(pl.multiple_of(r * 128, 128), 128), :]
+            tile = rows_of(v32, r).astype(BF16)
+            v[s, pl.ds(pl.multiple_of(r * 128, 128), 128), :] = tile
             m32[pl.ds(r, 128, stride=RH), :] = mm_nt(col[...], tile)
             return carry
 
-        lax.fori_loop(0, RH, column, 0)
+        widen_into(v32, vn.at[s])
+        lax.fori_loop(0, RH, column, 0, unroll=2)
         pack(0, s)
         if s == 0:
             pl.semaphore_wait(barrier, N_TILE - 1 + N_DP - 1)
@@ -149,7 +198,17 @@
         w32[at, :] = w16[at, :].astype(F32)
         return carry
 
-    lax.fori_loop(0, C, widen, 0)
+    lax.fori_loop(0, C, widen, 0, unroll=4)
+    loads[6].wait()
+    mix[...] = jnp.zeros_like(mix)
+    pointwise = l16[...].astype(F32)
+    mix[0, :64, :64] = pointwise.T
+    mix[0, 64:, 64:] = pointwise.T
+    mix[1, :64, :64] = pointwise
+    mix[1, 64:, 64:] = pointwise
+    loads[7].wait()
+    for s in range(S):
+        widen_into(ct.at[s], ctn.at[s])
 
     def spectrum(phase, s, scale):
         both = mm(fwd[...], rcv[phase, s])
@@ -172,14 +231,14 @@
         return lax.fori_loop(0, C, step, (zero, zero), unroll=4)
 
     def back_to_rows(phase, s, value, scale):
-        small = (value.astype(BF16).astype(F32) * scale).astype(BF16)
-        none = jnp.zeros_like(small)
+        small = value.astype(BF16).astype(F32) * scale
+        none = jnp.zeros((C, 128), F32)
         right = jnp.concatenate(
-            [jnp.concatenate([small, none], axis=1), jnp.concatenate([none, small], axis=1)], axis=0)
+            [jnp.concatenate([small, none], axis=1), jnp.concatenate([none, small], axis=1)], axis=0).T.astype(BF16)
 
         def rows(n, carry):
             at = pl.ds(pl.multiple_of(n * 256, 256), 256)
-            snd[phase, s, at, :] = mm_nt(inv[at, :], right).astype(BF16)
+            snd[phase, s, at, :] = mm(inv[at, :], right).astype(BF16)
             return carry
 
         lax.fori_loop(0, 4, rows, 0)
@@ -200,8 +259,6 @@
         return carry
 
     lax.fori_loop(0, C, swap, 0)
-    loads[6].wait()
-    loads[7].wait()
     lga[...] = jnp.zeros_like(lga)
 
     for s in range(S):
@@ -212,14 +269,14 @@
             at = pl.ds(pl.multiple_of(r * 128, 128), 128)
             spectral = b32[pl.ds(r, 128, stride=RH), :].T.astype(BF16)
             tile = v[s, at, :]
-            pre = mm(spectral, col[...]) + mm(mix[0], tile)
-            grad = (ct[s, at, :].astype(F32) * gelu_slope(pre)).astype(BF16)
+            pre = mm(spectral, col[...]) + mm(mix[0].astype(BF16), tile)
+            grad = (rows_of(ct.at[s], r) * gelu_slope(pre)).astype(BF16)
             gg[s, at, :] = grad
             m32[pl.ds(r, 128, stride=RH), :] = mm_nt(col[...], grad)
             lga[...] += mm_nt(tile, grad)
             return carry
 
-        lax.fori_loop(0, RH, gate, 0)
+        lax.fori_loop(0, RH, gate, 0, unroll=2)
         pack(2, s)
         exchange(2, s)
 
@@ -232,14 +289,12 @@
     lax.fori_loop(0, C, spread, 0)
 
     def send_rows(src_of, dst, n):
-        def send(i, carry):
-            p = partner(i)
+        def send(p):
             pltpu.make_async_remote_copy(
                 src_ref=src_of(p), dst_ref=dst.at[me], send_sem=lg_send.at[n], recv_sem=lg_recv.at[n],
                 device_id={"tile": p}, device_id_type=MESH).start()
-            return carry
-
-        lax.fori_loop(0, N_TILE - 1, send, 0)
+
+        to_others(send)
         pltpu.make_async_copy(src_of(me), dst.at[me], lg_recv.at[n]).start()
 
     send_rows(lambda p: lg1.at[p], lgr, 0)
@@ -287,27 +342,26 @@
         at = pl.multiple_of(c * 128, 128)
         mg[pl.ds(at, 64), :] = even
         mg[pl.ds(at + 64, 64), :] = odd
-        pltpu.make_async_copy(mg.at[pl.ds(at, 128), :], mg_hbm.at[pl.ds(at, 128), :], out_sem.at[0]).start()
         return carry
 
     lax.fori_loop(0, C // 2, outer, 0)
 
-    for s in range(S):
-        arrived(3, s)
-        b32[...] = rcv[3, s].astype(F32)
-
-        def back(r, carry):
-            at = pl.ds(pl.multiple_of(r * 128, 128), 128)
-            spectral = b32[pl.ds(r, 128, stride=RH), :].T.astype(BF16)
-            og[s, at, :] = (mm(spectral, col[...]) + mm(mix[1], gg[s, at, :])).astype(BF16)
-            pltpu.make_async_copy(og.at[s, at, :], og_hbm.at[s, at, :], out_sem.at[1]).start()
-            return carry
-
-        lax.fori_loop(0, RH, back, 0)
+    mixl[...] = mix[1].astype(BF16)
+    coll[...] = col[...]
+    ggl[...] = gg[1]
+    arrived(3, 0)
+    input_gradient(rcv.at[3, 0], gg.at[0], mixl, col, b32, v32, og)
 
     pltpu.make_async_copy(lgf, lgf, lg_recv.at[1]).wait()
-    tail = pltpu.make_async_copy(lgf, lg_hbm, out_sem.at[2])
-    tail.start()
+
+    def gather(c, carry):
+        lgs[pl.ds(c, 1), :] = lgf[c]
+        return carry
+
+    lax.fori_loop(0, C, gather, 0)
+    lg[...] = lgs[:, :C]
+    arrived(3, 1)
+    last[...] = rcv[3, 1]
 
     for phase in range(4):
         for s in range(S):
@@ -321,56 +375,66 @@
         pltpu.make_async_copy(sent, sent, lg_send.at[n]).wait()
     sent = lgd.at[pl.ds(0, N_DP - 1)]
     pltpu.make_async_copy(sent, sent, lg_send.at[2]).wait()
-    pltpu.make_async_copy(mg, mg_hbm, out_sem.at[0]).wait()
-    pltpu.make_async_copy(og, og_hbm, out_sem.at[1]).wait()
-    tail.wait()
 
 
 def step(inputs, cotangent, mode_weight, local_weight):
-    def row_major(field):
-        return jnp.swapaxes(field, 1, 2).reshape(S, TH * C, W)
-
-    paired = jnp.tile(local_weight, (2, 2))
-    same = jnp.asarray(np.kron(np.eye(2), np.ones((C, C))).astype(bool))
-    mixes = jnp.where(same[None], jnp.stack([paired.T, paired]), jnp.zeros((), BF16))
     rows = row_maps()
     col = jnp.asarray(column_rows(), BF16)
     inv = jnp.asarray(rows, BF16)
     fwd = jnp.asarray(np.ascontiguousarray(rows.T), BF16)
     dma = pltpu.SemaphoreType.DMA
     vm = pltpu.VMEM
-    og, mg, lg = pl.pallas_call(
+    here = pl.BlockSpec(memory_space=pltpu.VMEM)
+    anywhere = pl.BlockSpec(memory_space=pl.ANY)
+    ready = pl.pallas_call(
         kernel,
         out_shape=(
-            jax.ShapeDtypeStruct((S, TH * C, W), BF16),
+            jax.ShapeDtypeStruct((C * TH, W), BF16),
             jax.ShapeDtypeStruct((C * C, 2 * M1), F32),
-            jax.ShapeDtypeStruct((C, 1, 128), F32),
+            jax.ShapeDtypeStruct((C, C), F32),
+            jax.ShapeDtypeStruct((1024, 128), BF16),
+            jax.ShapeDtypeStruct((TH * C, W), BF16),
+            jax.ShapeDtypeStruct((128, 128), BF16),
+            jax.ShapeDtypeStruct((128, W), BF16),
         ),
-        in_specs=[pl.BlockSpec(memory_space=pl.ANY)] * 7,
-        out_specs=(pl.BlockSpec(memory_space=pl.ANY),) * 3,
+        in_specs=[anywhere] * 7,
+        out_specs=(here,) * 7,
         scratch_shapes=[
-            vm((S, TH * C, W), BF16), vm((S, TH * C, W), BF16),
+            vm((S, TH * C, W), BF16), vm((S, TH * C, W), BF16), vm((2, TH * C, 128), F32),
+            vm((S, TH * C, W), BF16), vm((S, 2, TH * C, 128), F32),
             vm((C * C, 128), BF16), vm((C * C, 128), F32), vm((C * C, 128), F32),
-            vm((2, 128, 128), BF16), vm((128, W), BF16), vm((1024, 256), BF16), vm((256, 1024), BF16),
+            vm((C, C), BF16), vm((2, 128, 128), F32), vm((128, W), BF16), vm((1024, 256), BF16), vm((256, 1024), BF16),
             vm((1024, 128), F32), vm((1024, 128), F32),
-            vm((S, TH * C, W), BF16), vm((S, TH * C, W), BF16),
+            vm((S, TH * C, W), BF16),
             vm((4, S, 1024, 128), BF16), vm((4, S, 1024, 128), BF16),
             vm((S, C, 128), BF16), vm((S, C, 128), BF16),
             vm((N_DP, S, C, 128), BF16), vm((N_DP, S, C, 128), BF16),
             vm((C, 128), F32), vm((C, 128), F32),
             vm((N_DP * S, C, 128), F32), vm((N_DP * S, C, 128), F32),
             vm((N_DP * S, C, 128), F32), vm((N_DP * S, C, 128), F32),
-            vm((C * C, 128), F32),
             vm((128, 128), F32), vm((C, 128), F32),
             vm((C, 1, 128), F32), vm((C, 1, 128), F32), vm((1, 1, 128), F32), vm((N_DP, 1, 128), F32),
             vm((1, 1, 128), F32), vm((C, 1, 128), F32),
-            dma((8,)), dma((4, S)), dma((4, S)), dma((2,)), dma((2,)), dma((3,)), dma((3,)), dma((3,)),
+            dma((8,)), dma((4, S)), dma((4, S)), dma((2,)), dma((2,)), dma((3,)), dma((3,)),
         ],
         compiler_params=pltpu.CompilerParams(
-            collective_id=0, has_side_effects=True, vmem_limit_bytes=48 << 20),
-    )(row_major(inputs), row_major(cotangent), mode_weight.reshape(C * C, 2 * M1), mixes, col, inv, fwd)
-    input_grad = jnp.swapaxes(og.reshape(S, TH, C, W), 1, 2)
-    return input_grad, mg.reshape(1, C, C, 2 * M1), lg[:, 0, :C]
+            collective_id=0, has_side_effects=True, vmem_limit_bytes=40 << 20),
+    )(*[pltpu.with_memory_space_constraint(a, pltpu.HBM) for a in (
+        inputs.reshape(S, C * TH, W), cotangent.reshape(S, C * TH, W), mode_weight.reshape(C * C, 2 * M1),
+        local_weight, col, inv, fwd)])
+    og, mg, lg = pl.pallas_call(
+        finish,
+        out_shape=(
+            jax.ShapeDtypeStruct((S, C * TH, W), BF16),
+            jax.ShapeDtypeStruct((C * C, 2 * M1), F32),
+            jax.ShapeDtypeStruct((C, C), F32),
+        ),
+        in_specs=[anywhere, anywhere, anywhere, here, here, here, here],
+        out_specs=(anywhere,) * 3,
+        scratch_shapes=[vm((1024, 128), F32), vm((2, TH * C, 128), F32), vm((C * TH, W), BF16), dma((4,))],
+        compiler_params=pltpu.CompilerParams(vmem_limit_bytes=8 << 20),
+    )(*ready)
+    return og.reshape(S, C, TH, W), mg.reshape(1, C, C, 2 * M1), lg
 
 
 def solution(mesh):

time: 77.9 us -> 66.6 us (0.85)
  local copies, waits for them, and re-layouts: 6.8 us -> 0 us
  Pallas kernels: 69.4 us -> 65.8 us
    pallas_call x1 -> x2, Pallas kernels: 69.4 us -> 65.8 us  [the longest x1 63.8 us: step(): pl.pallas_call(kernel, out_shape=(jax.ShapeDtypeStruct((C * TH, W), BF16)...]
    transpose x2 -> x0, local copies, waits for them, and re-layouts: 2.06 us -> none  [row_major(): return jnp.swapaxes(field, 1, 2).reshape(S, TH * C, W)]
    unnamed x14 -> x0, local copies, waits for them, and re-layouts: 2.04 us -> none
    reshape x1 -> x0, local copies, waits for them, and re-layouts: 1.55 us -> none  [step(): input_grad = jnp.swapaxes(og.reshape(S, TH, C, W), 1, 2)]
    another operation x4 -> x0, local copies, waits for them, and re-layouts: 1.15 us -> none  [the longest x3 1.05 us: step(): paired = jnp.tile(local_weight, (2, 2))]
where the time goes in v3:
time: 66.6 us; the launch traced here: 66.5 us
  Pallas kernels  65.8 us (99%)
    pallas_call x1, Pallas kernels, step(): pl.pallas_call(kernel, out_shape=(jax.ShapeDtypeStruct((C * TH, W), BF16)...  63.8 us
    pallas_call x1, Pallas kernels, step(): pl.pallas_call(finish, out_shape=(jax.ShapeDtypeStruct((S, C * TH, W), BF...  2.06 us

profile of v3, /device:TPU:1, one launch (start us, length us, event | category | flops | bytes accessed | tf_op | source)
XLA Modules:
  0.0 66.5 jit_solution(1808216693000070740)
XLA Ops:
  0.6 63.8 %shard_map.94 = (bf16[1024,256]{1,0:T(8,128)(2,1)S(1)}, f32[4096,128]{1,0:T(8,128)S(1)}, f32[64,64]{1,0:T(8,128)S(1)}, bf16[1024,128]{1,0:T(8,128)(2,1)S(1)}, bf...) custom-call(bf16[2,1024,256]{2,1,0:T(8,128)(2,1)} %bitcast.5, ...), custom_call_target="tpu_custom_call" | custom-call | tf_op jit(solution)/shard_map/pallas_call | solution.py:389
  64.4 2.1 %shard_map.95 = (bf16[2,1024,256]{2,1,0:T(8,128)(2,1)}, f32[4096,128]{1,0:T(8,128)}, f32[64,64]{1,0:T(8,128)}) custom-call(bf16[1024,256]{1,0:T(8,128)(2,1)S(1)} %get-tuple-element.13.og0, f32[4096,128]{1,0:T(8,128)S(1)} %get-tuple-element.14.mg, f32[64,64]{1,0:T(8,128)S(1)} %get-tuple-element.15.lg, bf16[1024,128]{1,0:T(8,128)(2,1)S(1)} %get-tuple-element.16.last, ...), custom_call_target="tpu_custom_call" | custom-call | tf_op jit(solution)/shard_map/pallas_call | solution.py:425

commit v4 on v3

--- a/solution.py
+++ b/solution.py
@@ -95,11 +95,12 @@
     my = lax.axis_index("dp")
     me_y, me_x, me_z = lax.div(me, 32), lax.rem(lax.div(me, 8), 4), lax.rem(me, 8)
 
-    column_of = [lax.rem(me_z + dz, 8) for dz in range(8)]
+    turn = 1 - 2 * lax.rem(me_z, 2)
+    column_of = [lax.rem(me_z + turn * dz + 8, 8) for dz in range(8)]
 
     def plane(k):
         kx = lax.rem(k, 4)
-        dx = 2 + (1 - 2 * lax.rem(kx, 2)) * lax.div(kx + 1, 2)
+        dx = lax.rem(1 + 2 * kx + lax.div(kx, 2), 4)
         dy = 1 - lax.div(k, 4)
         return lax.rem(me_y + dy, 2) * 32 + lax.rem(me_x + dx, 4) * 8
 
@@ -242,7 +243,6 @@
             return carry
 
         lax.fori_loop(0, 4, rows, 0)
-        exchange(phase, s)
 
     loads[3].wait()
     loads[5].wait()
@@ -253,6 +253,7 @@
         halves(xs[s])
         first, second = mix_rows(w32)
         back_to_rows(1, s, first - sgn * pltpu.roll(second, 64, 1), MODE)
+        exchange(1, s)
 
     def swap(o, carry):
         wt32[pl.ds(pl.multiple_of(o * 64, 64), 64), :] = w32[pl.ds(o, 64, stride=64), :]
@@ -260,6 +261,19 @@
 
     lax.fori_loop(0, C, swap, 0)
     lga[...] = jnp.zeros_like(lga)
+
+    def spread(c, carry):
+        lg1[c] = lgs[pl.ds(c, 1), :]
+        return carry
+
+    def send_rows(src_of, dst, n):
+        def send(p):
+            pltpu.make_async_remote_copy(
+                src_ref=src_of(p), dst_ref=dst.at[me], send_sem=lg_send.at[n], recv_sem=lg_recv.at[n],
+                device_id={"tile": p}, device_id_type=MESH).start()
+
+        to_others(send)
+        pltpu.make_async_copy(src_of(me), dst.at[me], lg_recv.at[n]).start()
 
     for s in range(S):
         arrived(1, s)
@@ -278,26 +292,11 @@
 
         lax.fori_loop(0, RH, gate, 0, unroll=2)
         pack(2, s)
+        if s == S - 1:
+            lgs[...] = lga[:64] + pltpu.roll(lga[64:], 64, 1)
+            lax.fori_loop(0, C, spread, 0, unroll=4)
+            send_rows(lambda p: lg1.at[p], lgr, 0)
         exchange(2, s)
-
-    lgs[...] = lga[:64] + pltpu.roll(lga[64:], 64, 1)
-
-    def spread(c, carry):
-        lg1[c] = lgs[pl.ds(c, 1), :]
-        return carry
-
-    lax.fori_loop(0, C, spread, 0)
-
-    def send_rows(src_of, dst, n):
-        def send(p):
-            pltpu.make_async_remote_copy(
-                src_ref=src_of(p), dst_ref=dst.at[me], send_sem=lg_send.at[n], recv_sem=lg_recv.at[n],
-                device_id={"tile": p}, device_id_type=MESH).start()
-
-        to_others(send)
-        pltpu.make_async_copy(src_of(me), dst.at[me], lg_recv.at[n]).start()
-
-    send_rows(lambda p: lg1.at[p], lgr, 0)
 
     for s in range(S):
         arrived(2, s)
@@ -306,14 +305,20 @@
         halves(ds[s])
         first, second = mix_rows(wt32)
         back_to_rows(3, s, pltpu.roll(second, 64, 1) + sgn * first, SPEC)
-
-    pltpu.make_async_copy(lgr, lgr, lg_recv.at[0]).wait()
-    lgp[0] = jnp.sum(lgr[...], axis=0)
-    for j in range(1, N_DP):
-        pltpu.make_async_remote_copy(
-            src_ref=lgp.at[0], dst_ref=lgd.at[my], send_sem=lg_send.at[2], recv_sem=lg_recv.at[2],
-            device_id={"dp": group(j)}, device_id_type=MESH).start()
-    pltpu.make_async_copy(lgp.at[0], lgd.at[my], lg_recv.at[2]).start()
+        if s == 0:
+            pltpu.make_async_copy(lgr, lgr, lg_recv.at[0]).wait()
+            lgp[0] = jnp.sum(lgr[...], axis=0)
+            for j in range(1, N_DP):
+                pltpu.make_async_remote_copy(
+                    src_ref=lgp.at[0], dst_ref=lgd.at[my], send_sem=lg_send.at[2], recv_sem=lg_recv.at[2],
+                    device_id={"dp": group(j)}, device_id_type=MESH).start()
+            pltpu.make_async_copy(lgp.at[0], lgd.at[my], lg_recv.at[2]).start()
+        else:
+            pltpu.make_async_copy(lgd, lgd, lg_recv.at[2]).wait()
+            lge[0] = jnp.sum(lgd[...], axis=0)
+            send_rows(lambda p: lge.at[0], lgf, 1)
+        exchange(3, s)
+
 
     pltpu.make_async_copy(xall, xall, dp_recv.at[0]).wait()
     pltpu.make_async_copy(dall, dall, dp_recv.at[1]).wait()
@@ -327,10 +332,6 @@
             grad = dall[g, s].astype(F32)
             d1[n] = grad
             d2[n] = pltpu.roll(grad, 64, 1)
-
-    pltpu.make_async_copy(lgd, lgd, lg_recv.at[2]).wait()
-    lge[0] = jnp.sum(lgd[...], axis=0)
-    send_rows(lambda p: lge.at[0], lgf, 1)
 
     def outer(c, carry):
         even = jnp.zeros((C, 128), F32)

time: 66.6 us -> 65.2 us (0.979)
  Pallas kernels: 65.8 us -> 64.1 us
    pallas_call x1, Pallas kernels: 63.8 us -> 62.1 us  [step(): pl.pallas_call(kernel, out_shape=(jax.ShapeDtypeStruct((C * TH, W), BF16)...]
where the time goes in v4:
time: 65.2 us; the launch traced here: 64.8 us
  Pallas kernels  64.1 us (98%)
    pallas_call x1, Pallas kernels, step(): pl.pallas_call(kernel, out_shape=(jax.ShapeDtypeStruct((C * TH, W), BF16)...  62.1 us
    pallas_call x1, Pallas kernels, step(): pl.pallas_call(finish, out_shape=(jax.ShapeDtypeStruct((S, C * TH, W), BF...  2.06 us

profile of v4, /device:TPU:1, one launch (start us, length us, event | category | flops | bytes accessed | tf_op | source)
XLA Modules:
  0.0 64.8 jit_solution(10398074601910885625)
XLA Ops:
  0.6 62.1 %shard_map.94 = (bf16[1024,256]{1,0:T(8,128)(2,1)S(1)}, f32[4096,128]{1,0:T(8,128)S(1)}, f32[64,64]{1,0:T(8,128)S(1)}, bf16[1024,128]{1,0:T(8,128)(2,1)S(1)}, bf...) custom-call(bf16[2,1024,256]{2,1,0:T(8,128)(2,1)} %bitcast.5, ...), custom_call_target="tpu_custom_call" | custom-call | tf_op jit(solution)/shard_map/pallas_call | solution.py:390
  62.7 2.1 %shard_map.95 = (bf16[2,1024,256]{2,1,0:T(8,128)(2,1)}, f32[4096,128]{1,0:T(8,128)}, f32[64,64]{1,0:T(8,128)}) custom-call(bf16[1024,256]{1,0:T(8,128)(2,1)S(1)} %get-tuple-element.13.og0, f32[4096,128]{1,0:T(8,128)S(1)} %get-tuple-element.14.mg, f32[64,64]{1,0:T(8,128)S(1)} %get-tuple-element.15.lg, bf16[1024,128]{1,0:T(8,128)(2,1)S(1)} %get-tuple-element.16.last, ...), custom_call_target="tpu_custom_call" | custom-call | tf_op jit(solution)/shard_map/pallas_call | solution.py:426

commit v5 on v4

--- a/solution.py
+++ b/solution.py
@@ -68,7 +68,7 @@
                 wide[half, pl.ds(2 * r + n, C, stride=TH), :] = value[n * C:(n + 1) * C, half * 128:(half + 1) * 128]
         return carry
 
-    lax.fori_loop(0, RH, back, 0, unroll=2)
+    lax.fori_loop(0, RH, back, 0, unroll=4)
     for half in range(2):
         result[:, half * 128:(half + 1) * 128] = wide[half].astype(BF16)
 
@@ -89,7 +89,7 @@
 def kernel(v_hbm, ct_hbm, w_hbm, l_hbm, col_hbm, inv_hbm, fwd_hbm,
            og, mg, lg, last, ggl, mixl, coll,
            v, vn, v32, ctn, ct, w16, w32, wt32, l16, mix, col, inv, fwd, m32, b32, gg, snd, rcv,
-           xs, ds, xall, dall, pa, pb, x1, x2, d1, d2, lga, lgs, lg1, lgr, lgp, lgd, lge, lgf,
+           xs, ds, xall, dall, pa, pb, x1, x2, d1, d2, lga, lgs, lgd, lgp, lgr, lge, lgz, lgq, lgf,
            load_sem, send_sem, recv_sem, dp_send, dp_recv, lg_send, lg_recv):
     me = lax.axis_index("tile")
     my = lax.axis_index("dp")
@@ -186,7 +186,7 @@
             return carry
 
         widen_into(v32, vn.at[s])
-        lax.fori_loop(0, RH, column, 0, unroll=2)
+        lax.fori_loop(0, RH, column, 0, unroll=4)
         pack(0, s)
         if s == 0:
             pl.semaphore_wait(barrier, N_TILE - 1 + N_DP - 1)
@@ -229,7 +229,7 @@
             return first + pa[pl.ds(c, 1), :] * block, second + pb[pl.ds(c, 1), :] * block
 
         zero = jnp.zeros((C, 128), F32)
-        return lax.fori_loop(0, C, step, (zero, zero), unroll=4)
+        return lax.fori_loop(0, C, step, (zero, zero), unroll=8)
 
     def back_to_rows(phase, s, value, scale):
         small = value.astype(BF16).astype(F32) * scale
@@ -242,18 +242,18 @@
             snd[phase, s, at, :] = mm(inv[at, :], right).astype(BF16)
             return carry
 
-        lax.fori_loop(0, 4, rows, 0)
+        lax.fori_loop(0, 4, rows, 0, unroll=4)
 
     loads[3].wait()
     loads[5].wait()
     for s in range(S):
         arrived(0, s)
         xs[s] = spectrum(0, s, SPEC)
-        to_group(xs, xall, s, 0)
         halves(xs[s])
         first, second = mix_rows(w32)
         back_to_rows(1, s, first - sgn * pltpu.roll(second, 64, 1), MODE)
         exchange(1, s)
+        to_group(xs, xall, s, 0)
 
     def swap(o, carry):
         wt32[pl.ds(pl.multiple_of(o * 64, 64), 64), :] = w32[pl.ds(o, 64, stride=64), :]
@@ -262,18 +262,47 @@
     lax.fori_loop(0, C, swap, 0)
     lga[...] = jnp.zeros_like(lga)
 
-    def spread(c, carry):
-        lg1[c] = lgs[pl.ds(c, 1), :]
-        return carry
-
-    def send_rows(src_of, dst, n):
-        def send(p):
+    my_plane = lax.div(me, 8)
+
+    def to_plane(src_of, dst, n):
+        for k in range(1, 8):
+            other = lax.rem(me_y + k // 4, 2) * 4 + lax.rem(me_x + k % 4, 4)
             pltpu.make_async_remote_copy(
-                src_ref=src_of(p), dst_ref=dst.at[me], send_sem=lg_send.at[n], recv_sem=lg_recv.at[n],
-                device_id={"tile": p}, device_id_type=MESH).start()
-
-        to_others(send)
-        pltpu.make_async_copy(src_of(me), dst.at[me], lg_recv.at[n]).start()
+                src_ref=src_of(other), dst_ref=dst.at[my_plane], send_sem=lg_send.at[n], recv_sem=lg_recv.at[n],
+                device_id={"tile": other * 8 + me_z}, device_id_type=MESH).start()
+        pltpu.make_async_copy(src_of(my_plane), dst.at[my_plane], lg_recv.at[n]).start()
+
+    def collected(ref, n):
+        pltpu.make_async_copy(ref, ref, lg_recv.at[n]).wait()
+
+    def point_hop(n):
+        if n == 0:
+            lgs[...] = lga[:64] + pltpu.roll(lga[64:], 64, 1)
+            for j in range(1, N_DP):
+                pltpu.make_async_remote_copy(
+                    src_ref=lgs, dst_ref=lgd.at[my], send_sem=lg_send.at[0], recv_sem=lg_recv.at[0],
+                    device_id={"dp": group(j)}, device_id_type=MESH).start()
+            pltpu.make_async_copy(lgs, lgd.at[my], lg_recv.at[0]).start()
+        elif n == 1:
+            collected(lgd, 0)
+            lgp[...] = jnp.sum(lgd[...], axis=0).reshape(8, 8, 128)
+            to_plane(lambda other: lgp.at[other], lgr, 1)
+        elif n == 2:
+            collected(lgr, 1)
+            lge[...] = jnp.sum(lgr[...], axis=0)
+            for dz in range(1, 8):
+                z = lax.rem(me_z + dz, 8)
+                pltpu.make_async_remote_copy(
+                    src_ref=lge, dst_ref=lgz.at[me_z], send_sem=lg_send.at[2], recv_sem=lg_recv.at[2],
+                    device_id={"tile": me - me_z + z}, device_id_type=MESH).start()
+            pltpu.make_async_copy(lge, lgz.at[me_z], lg_recv.at[2]).start()
+        elif n == 3:
+            collected(lgz, 2)
+            lgq[...] = jnp.sum(lgz[...], axis=0)
+            to_plane(lambda other: lgq, lgf, 3)
+        else:
+            collected(lgf, 3)
+            lg[...] = lgf[...].reshape(C, 128)[:, :C]
 
     for s in range(S):
         arrived(1, s)
@@ -290,12 +319,10 @@
             lga[...] += mm_nt(tile, grad)
             return carry
 
-        lax.fori_loop(0, RH, gate, 0, unroll=2)
+        lax.fori_loop(0, RH, gate, 0, unroll=4)
         pack(2, s)
         if s == S - 1:
-            lgs[...] = lga[:64] + pltpu.roll(lga[64:], 64, 1)
-            lax.fori_loop(0, C, spread, 0, unroll=4)
-            send_rows(lambda p: lg1.at[p], lgr, 0)
+            point_hop(0)
         exchange(2, s)
 
     for s in range(S):
@@ -305,18 +332,7 @@
         halves(ds[s])
         first, second = mix_rows(wt32)
         back_to_rows(3, s, pltpu.roll(second, 64, 1) + sgn * first, SPEC)
-        if s == 0:
-            pltpu.make_async_copy(lgr, lgr, lg_recv.at[0]).wait()
-            lgp[0] = jnp.sum(lgr[...], axis=0)
-            for j in range(1, N_DP):
-                pltpu.make_async_remote_copy(
-                    src_ref=lgp.at[0], dst_ref=lgd.at[my], send_sem=lg_send.at[2], recv_sem=lg_recv.at[2],
-                    device_id={"dp": group(j)}, device_id_type=MESH).start()
-            pltpu.make_async_copy(lgp.at[0], lgd.at[my], lg_recv.at[2]).start()
-        else:
-            pltpu.make_async_copy(lgd, lgd, lg_recv.at[2]).wait()
-            lge[0] = jnp.sum(lgd[...], axis=0)
-            send_rows(lambda p: lge.at[0], lgf, 1)
+        point_hop(1 + s)
         exchange(3, s)
 
 
@@ -346,6 +362,7 @@
         return carry
 
     lax.fori_loop(0, C // 2, outer, 0)
+    point_hop(3)
 
     mixl[...] = mix[1].astype(BF16)
     coll[...] = col[...]
@@ -353,14 +370,7 @@
     arrived(3, 0)
     input_gradient(rcv.at[3, 0], gg.at[0], mixl, col, b32, v32, og)
 
-    pltpu.make_async_copy(lgf, lgf, lg_recv.at[1]).wait()
-
-    def gather(c, carry):
-        lgs[pl.ds(c, 1), :] = lgf[c]
-        return carry
-
-    lax.fori_loop(0, C, gather, 0)
-    lg[...] = lgs[:, :C]
+    point_hop(4)
     arrived(3, 1)
     last[...] = rcv[3, 1]
 
@@ -371,11 +381,9 @@
     for n, ref in ((0, xall), (1, dall)):
         sent = ref.at[pl.ds(0, N_DP - 1)]
         pltpu.make_async_copy(sent, sent, dp_send.at[n]).wait()
-    for n in range(2):
-        sent = lgr.at[pl.ds(0, N_TILE - 1)]
+    for n, ref, count in ((0, lgd, N_DP), (1, lgr, 8), (2, lgz, 8), (3, lgf, 8)):
+        sent = ref.at[pl.ds(0, count - 1)]
         pltpu.make_async_copy(sent, sent, lg_send.at[n]).wait()
-    sent = lgd.at[pl.ds(0, N_DP - 1)]
-    pltpu.make_async_copy(sent, sent, lg_send.at[2]).wait()
 
 
 def step(inputs, cotangent, mode_weight, local_weight):
@@ -414,9 +422,9 @@
             vm((N_DP * S, C, 128), F32), vm((N_DP * S, C, 128), F32),
             vm((N_DP * S, C, 128), F32), vm((N_DP * S, C, 128), F32),
             vm((128, 128), F32), vm((C, 128), F32),
-            vm((C, 1, 128), F32), vm((C, 1, 128), F32), vm((1, 1, 128), F32), vm((N_DP, 1, 128), F32),
-            vm((1, 1, 128), F32), vm((C, 1, 128), F32),
-            dma((8,)), dma((4, S)), dma((4, S)), dma((2,)), dma((2,)), dma((3,)), dma((3,)),
+            vm((N_DP, C, 128), F32), vm((8, 8, 128), F32), vm((8, 8, 128), F32),
+            vm((8, 128), F32), vm((8, 8, 128), F32), vm((8, 128), F32), vm((8, 8, 128), F32),
+            dma((8,)), dma((4, S)), dma((4, S)), dma((2,)), dma((2,)), dma((4,)), dma((4,)),
         ],
         compiler_params=pltpu.CompilerParams(
             collective_id=0, has_side_effects=True, vmem_limit_bytes=40 << 20),

time: 65.2 us -> 64.4 us (0.988)
  no operation moved by 1% of the time
where the time goes in v5:
time: 64.4 us; the launch traced here: 64.3 us
  Pallas kernels  63.7 us (99%)
    pallas_call x1, Pallas kernels, step(): pl.pallas_call(kernel, out_shape=(jax.ShapeDtypeStruct((C * TH, W), BF16)...  62 us
    pallas_call x1, Pallas kernels, step(): pl.pallas_call(finish, out_shape=(jax.ShapeDtypeStruct((S, C * TH, W), BF...  1.71 us

profile of v5, /device:TPU:1, one launch (start us, length us, event | category | flops | bytes accessed | tf_op | source)
XLA Modules:
  0.0 64.3 jit_solution(9165726914125306439)
XLA Ops:
  0.6 62.0 %shard_map.94 = (bf16[1024,256]{1,0:T(8,128)(2,1)S(1)}, f32[4096,128]{1,0:T(8,128)S(1)}, f32[64,64]{1,0:T(8,128)S(1)}, bf16[1024,128]{1,0:T(8,128)(2,1)S(1)}, bf...) custom-call(bf16[2,1024,256]{2,1,0:T(8,128)(2,1)} %bitcast.5, ...), custom_call_target="tpu_custom_call" | custom-call | tf_op jit(solution)/shard_map/pallas_call | solution.py:398
  62.6 1.7 %shard_map.95 = (bf16[2,1024,256]{2,1,0:T(8,128)(2,1)}, f32[4096,128]{1,0:T(8,128)}, f32[64,64]{1,0:T(8,128)}) custom-call(bf16[1024,256]{1,0:T(8,128)(2,1)S(1)} %get-tuple-element.13.og0, f32[4096,128]{1,0:T(8,128)S(1)} %get-tuple-element.14.mg, f32[64,64]{1,0:T(8,128)S(1)} %get-tuple-element.15.lg, bf16[1024,128]{1,0:T(8,128)(2,1)S(1)} %get-tuple-element.16.last, ...), custom_call_target="tpu_custom_call" | custom-call | tf_op jit(solution)/shard_map/pallas_call | solution.py:434

commit v6 on v5

--- a/solution.py
+++ b/solution.py
@@ -57,38 +57,52 @@
     return cumulative + values * density
 
 
-def input_gradient(received, grad, mix, col, b32, wide, result):
-    b32[...] = received[...].astype(F32)
-
-    def back(r, carry):
-        spectral = b32[pl.ds(r, 128, stride=RH), :].T.astype(BF16)
-        value = mm(spectral, col[...]) + mm(mix[...], grad[pl.ds(pl.multiple_of(r * 128, 128), 128), :])
+def pointwise_part(grad, mix, wide):
+    def part(r, carry):
+        value = mm(mix[...], grad[pl.ds(pl.multiple_of(r * 128, 128), 128), :])
         for n in range(RL):
             for half in range(2):
                 wide[half, pl.ds(2 * r + n, C, stride=TH), :] = value[n * C:(n + 1) * C, half * 128:(half + 1) * 128]
         return carry
 
-    lax.fori_loop(0, RH, back, 0, unroll=4)
-    for half in range(2):
-        result[:, half * 128:(half + 1) * 128] = wide[half].astype(BF16)
-
-
-def finish(og0, mg, lg, last, ggl, mixl, coll, og_hbm, mg_hbm, lg_hbm, b32, wide, og1, sem):
+    lax.fori_loop(0, RH, part, 0, unroll=4)
+
+
+def input_gradient(received, wide, col, b32, t32, result, done):
+    b32[...] = received[...].astype(F32)
+
+    def turn(r, carry):
+        value = b32[pl.ds(r, 128, stride=RH), :].T
+        for n in range(RL):
+            t32[pl.ds(2 * r + n, C, stride=TH), :] = value[n * C:(n + 1) * C]
+        return carry
+
+    lax.fori_loop(0, RH, turn, 0, unroll=4)
+    for n in range(4):
+        at = slice(n * 256, (n + 1) * 256)
+        value = mm(t32[at, :].astype(BF16), col[...])
+        for half in range(2):
+            lanes = slice(half * 128, (half + 1) * 128)
+            result[at, lanes] = (value[:, lanes] + wide[half, at, :]).astype(BF16)
+        done(n)
+
+
+def finish(og0, mg, lg, last, wide, coll, og_hbm, mg_hbm, lg_hbm, b32, t32, og1, sem):
     copies = [
         pltpu.make_async_copy(a, b, sem.at[n])
-        for n, (a, b) in enumerate([(mg, mg_hbm), (og0, og_hbm.at[0]), (lg, lg_hbm), (og1, og_hbm.at[1])])
+        for n, (a, b) in enumerate([(mg, mg_hbm), (og0, og_hbm.at[0]), (lg, lg_hbm)] + [
+            (og1.at[pl.ds(256 * n, 256), :], og_hbm.at[1, pl.ds(256 * n, 256), :]) for n in range(4)])
     ]
     for copy in copies[:3]:
         copy.start()
-    input_gradient(last, ggl, mixl, coll, b32, wide, og1)
-    copies[3].start()
+    input_gradient(last, wide, coll, b32, t32, og1, lambda n: copies[3 + n].start())
     for copy in copies:
         copy.wait()
 
 
 def kernel(v_hbm, ct_hbm, w_hbm, l_hbm, col_hbm, inv_hbm, fwd_hbm,
-           og, mg, lg, last, ggl, mixl, coll,
-           v, vn, v32, ctn, ct, w16, w32, wt32, l16, mix, col, inv, fwd, m32, b32, gg, snd, rcv,
+           og, mg, lg, last, wide1, coll,
+           v, vn, v32, ctn, ct, w16, w32, wt32, l16, mix, col, inv, fwd, m32, b32, t32, mixl, gg, snd, rcv,
            xs, ds, xall, dall, pa, pb, x1, x2, d1, d2, lga, lgs, lgd, lgp, lgr, lge, lgz, lgq, lgf,
            load_sem, send_sem, recv_sem, dp_send, dp_recv, lg_send, lg_recv):
     me = lax.axis_index("tile")
@@ -366,9 +380,10 @@
 
     mixl[...] = mix[1].astype(BF16)
     coll[...] = col[...]
-    ggl[...] = gg[1]
+    pointwise_part(gg.at[0], mixl, v32)
+    pointwise_part(gg.at[1], mixl, wide1)
     arrived(3, 0)
-    input_gradient(rcv.at[3, 0], gg.at[0], mixl, col, b32, v32, og)
+    input_gradient(rcv.at[3, 0], v32, col, b32, t32, og, lambda n: None)
 
     point_hop(4)
     arrived(3, 1)
@@ -402,18 +417,17 @@
             jax.ShapeDtypeStruct((C * C, 2 * M1), F32),
             jax.ShapeDtypeStruct((C, C), F32),
             jax.ShapeDtypeStruct((1024, 128), BF16),
-            jax.ShapeDtypeStruct((TH * C, W), BF16),
-            jax.ShapeDtypeStruct((128, 128), BF16),
+            jax.ShapeDtypeStruct((2, TH * C, 128), F32),
             jax.ShapeDtypeStruct((128, W), BF16),
         ),
         in_specs=[anywhere] * 7,
-        out_specs=(here,) * 7,
+        out_specs=(here,) * 6,
         scratch_shapes=[
             vm((S, TH * C, W), BF16), vm((S, TH * C, W), BF16), vm((2, TH * C, 128), F32),
             vm((S, TH * C, W), BF16), vm((S, 2, TH * C, 128), F32),
             vm((C * C, 128), BF16), vm((C * C, 128), F32), vm((C * C, 128), F32),
             vm((C, C), BF16), vm((2, 128, 128), F32), vm((128, W), BF16), vm((1024, 256), BF16), vm((256, 1024), BF16),
-            vm((1024, 128), F32), vm((1024, 128), F32),
+            vm((1024, 128), F32), vm((1024, 128), F32), vm((1024, 128), F32), vm((128, 128), BF16),
             vm((S, TH * C, W), BF16),
             vm((4, S, 1024, 128), BF16), vm((4, S, 1024, 128), BF16),
             vm((S, C, 128), BF16), vm((S, C, 128), BF16),
@@ -438,9 +452,9 @@
             jax.ShapeDtypeStruct((C * C, 2 * M1), F32),
             jax.ShapeDtypeStruct((C, C), F32),
         ),
-        in_specs=[anywhere, anywhere, anywhere, here, here, here, here],
+        in_specs=[anywhere, anywhere, anywhere, here, here, here],
         out_specs=(anywhere,) * 3,
-        scratch_shapes=[vm((1024, 128), F32), vm((2, TH * C, 128), F32), vm((C * TH, W), BF16), dma((4,))],
+        scratch_shapes=[vm((1024, 128), F32), vm((1024, 128), F32), vm((C * TH, W), BF16), dma((7,))],
         compiler_params=pltpu.CompilerParams(vmem_limit_bytes=8 << 20),
     )(*ready)
     return og.reshape(S, C, TH, W), mg.reshape(1, C, C, 2 * M1), lg

time: 64.4 us -> 64.4 us (level)
  no operation moved by 1% of the time
where the time goes in v6:
time: 64.4 us; the launch traced here: 64.3 us
  Pallas kernels  63.7 us (99%)
    pallas_call x1, Pallas kernels, step(): pl.pallas_call(kernel, out_shape=(jax.ShapeDtypeStruct((C * TH, W), BF16)...  62 us
    pallas_call x1, Pallas kernels, step(): pl.pallas_call(finish, out_shape=(jax.ShapeDtypeStruct((S, C * TH, W), BF...  1.72 us

profile of v6, /device:TPU:1, one launch (start us, length us, event | category | flops | bytes accessed | tf_op | source)
XLA Modules:
  0.0 64.3 jit_solution(4771324246762961435)
XLA Ops:
  0.6 62.0 %shard_map.94 = (bf16[1024,256]{1,0:T(8,128)(2,1)S(1)}, f32[4096,128]{1,0:T(8,128)S(1)}, f32[64,64]{1,0:T(8,128)S(1)}, bf16[1024,128]{1,0:T(8,128)(2,1)S(1)}, f3...) custom-call(bf16[2,1024,256]{2,1,0:T(8,128)(2,1)} %bitcast.5, bf16[2,1024,256]{2,1,0:T(8,128)(2,1)} %bitcast.6, ...), custom_call_target="tpu_custom_call" | custom-call | tf_op jit(solution)/shard_map/pallas_call | solution.py:413
  62.6 1.7 %shard_map.95 = (bf16[2,1024,256]{2,1,0:T(8,128)(2,1)}, f32[4096,128]{1,0:T(8,128)}, f32[64,64]{1,0:T(8,128)}) custom-call(bf16[1024,256]{1,0:T(8,128)(2,1)S(1)} %get-tuple-element.12.og0, f32[4096,128]{1,0:T(8,128)S(1)} %get-tuple-element.13.mg, f32[64,64]{1,0:T(8,128)S(1)} %get-tuple-element.14.lg, bf16[1024,128]{1,0:T(8,128)(2,1)S(1)} %get-tuple-element.15.last, ...), custom_call_target="tpu_custom_call" | custom-call | tf_op jit(solution)/shard_map/pallas_call | solution.py:448
